TPU v7x, 256 devices: a whole 4x4x8 slice. The times are simulated.
256 devices in a mesh: blk: 64 (over y, z_hi, x), tp: 4 (over z_lo, core).
Axes of the slice: x: 4, y: 4, z: 8 (z_hi: 4, z_lo: 2; z = z_hi * 2 + z_lo), core: 2. Of those that a mesh axis runs over, the one named last changes fastest.
Arguments:
- hidden_in: bfloat16 [8192, 5120], P(('blk', 'tp')), may hold values from -6 to 6
- norm_gain: bfloat16 [5120], replicated, may hold values from 0.099609375 to 1.8984375
- kv_weight: bfloat16 [5120, 2, 1024], P(None, None, 'tp'), may hold values from -0.078125 to 0.078125
- kv_bias: bfloat16 [2, 1024], P(None, 'tp'), may hold values from -3 to 3
- queries: bfloat16 [8192, 5120], P('blk', 'tp'), may hold values from -110 to 110
- cache_pages: bfloat16 [64, 128, 2, 8, 128], P('blk', None, None, 'tp'), may hold values from -6 to 6
- out_weight: bfloat16 [5120, 5120], P('tp', 'blk'), may hold values from -0.3125 to 0.3125
- cached_len: int32 [64], replicated, may hold values from 0 to 4096
- page_table: int32 [64, 32], replicated, may hold values from 0 to 63, as said below
Outputs:
- hidden_out: bfloat16 [8192, 5120], P(('blk', 'tp'))
- new_kv: bfloat16 [8192, 2, 8, 128], P('blk', None, 'tp')
Inputs may be any that keep to these rules, and one draw needn't show every extreme that they name: `page_table`: request r's cache fills its first ceil(cached_len[r] / 128) page table entries with distinct physical pages, no page serving two requests; later entries are 0. One request holds exactly 4096 tokens.
All inputs are finite; a program needn't handle non-finite values.
Results may differ from a plain program's by a relative error of at most 0.012.
The roundings to bfloat16 on the way count: a program that leaves them out, or rounds other values in their place, can miss the bound.
Values may be sent and summed in bfloat16 or wider, within the bound.
A program may use at most 128 MiB of HBM per device.

v0:
```python
import jax
import jax.numpy as jnp
from jax import lax
from jax.sharding import PartitionSpec as P

EPS = 1e-06
THETA = 1000000.0


def from_behind(array, axis, by):
    devices = lax.axis_size(axis)
    return lax.ppermute(array, axis, [(i, (i + by) % devices) for i in range(devices)])


def rotate(values, positions, head_dim):
    half_dim = head_dim // 2
    inverse = jnp.power(THETA, -jnp.arange(half_dim, dtype=jnp.float32) * 2.0 / head_dim)
    angles = positions[:, None] * inverse[None, :]
    cosine = jnp.cos(angles)[:, None, :]
    sine_val = jnp.sin(angles)[:, None, :]
    front_half = values[..., :half_dim]
    back_half = values[..., half_dim:]
    return jnp.concatenate(
        [front_half * cosine - back_half * sine_val, back_half * cosine + front_half * sine_val],
        axis=-1,
    )


def attend(running, query_rot, key_rows, value_rows, visible, score_scale):
    row_max, row_sum, weighted = running
    scores = (
        jnp.einsum("tkgd,nkd->kgtn", query_rot, key_rows, preferred_element_type=jnp.float32)
        * score_scale
    )
    masked = jnp.where(visible[None, None], scores, -jnp.inf)
    new_max = jnp.maximum(row_max, jnp.max(masked, axis=-1))
    rescale = jnp.exp(row_max - new_max)
    weights = jnp.exp(masked - new_max[..., None])
    new_sum = row_sum * rescale + jnp.sum(weights, axis=-1)
    update = jnp.einsum(
        "kgtn,nkd->kgtd",
        weights.astype(jnp.bfloat16),
        value_rows,
        preferred_element_type=jnp.float32,
    )
    return (new_max, new_sum, weighted * rescale[..., None] + update)


def local(
    hidden_in,
    norm_gain,
    kv_weight,
    kv_bias,
    queries,
    cache_pages,
    out_weight,
    cached_len,
    page_table,
):
    head_dim = cache_pages.shape[4]
    heads_kv = cache_pages.shape[3]
    page_len = cache_pages.shape[1]
    pages_dev = cache_pages.shape[0]
    tok_rows = queries.shape[0]
    heads_q = queries.shape[1] // head_dim
    group_size = heads_q // heads_kv
    score_scale = head_dim ** (-0.5)
    hidden_f = hidden_in.astype(jnp.float32)
    inverse_rms = lax.rsqrt(jnp.mean(hidden_f * hidden_f, axis=-1, keepdims=True) + EPS)
    normed = (hidden_f * inverse_rms * norm_gain.astype(jnp.float32)).astype(jnp.bfloat16)
    rows_all = lax.all_gather(normed, "tp", axis=0, tiled=True)
    blk_index = lax.axis_index("blk")
    length = cached_len[blk_index]
    positions = (length + jnp.arange(tok_rows, dtype=jnp.int32)).astype(jnp.float32)
    kv_proj = jnp.einsum(
        "td,dsc->tsc", rows_all, kv_weight, preferred_element_type=jnp.float32
    ) + kv_bias.astype(jnp.float32)
    kv_proj = kv_proj.reshape(tok_rows, 2, heads_kv, head_dim)
    key_rot = rotate(kv_proj[:, 0], positions, head_dim)
    new_pair = jnp.stack([key_rot, kv_proj[:, 1]], axis=1).astype(jnp.bfloat16)
    query_rot = rotate(
        queries.astype(jnp.float32).reshape(tok_rows, heads_q, head_dim), positions, head_dim
    )
    query_rot = query_rot.astype(jnp.bfloat16).reshape(tok_rows, heads_kv, group_size, head_dim)
    running = (
        jnp.full((heads_kv, group_size, tok_rows), -jnp.inf, jnp.float32),
        jnp.zeros((heads_kv, group_size, tok_rows), jnp.float32),
        jnp.zeros((heads_kv, group_size, tok_rows, head_dim), jnp.float32),
    )
    token_ids = jnp.arange(tok_rows, dtype=jnp.int32)
    causal = token_ids[None, :] <= token_ids[:, None]
    running = attend(running, query_rot, new_pair[:, 0], new_pair[:, 1], causal, score_scale)
    page_row = page_table[blk_index]
    live_count = (length + page_len - 1) // page_len
    slot_ids = jnp.arange(page_row.shape[0], dtype=jnp.int32)
    within_page = jnp.arange(page_len, dtype=jnp.int32)

    def visit_pages(state_now, block_pages, first_page):

        def visit_one(page_slot, inner_state):
            page_data = lax.dynamic_index_in_dim(block_pages, page_slot, 0, keepdims=False)
            matches = (page_row == first_page + page_slot) & (slot_ids < live_count)
            logical = jnp.sum(jnp.where(matches, slot_ids, 0))
            visible = (logical * page_len + within_page < length)[None, :]
            return lax.cond(
                jnp.any(matches),
                lambda inner: attend(
                    inner, query_rot, page_data[:, 0], page_data[:, 1], visible, score_scale
                ),
                lambda inner: inner,
                inner_state,
            )

        return lax.fori_loop(0, block_pages.shape[0], visit_one, state_now)

    blk_count = lax.axis_size("blk")
    running = visit_pages(running, cache_pages, blk_index * pages_dev)

    def cycle_step(step_index, loop_state):
        state_now, travelling = loop_state
        travelling = from_behind(travelling, "blk", 1)
        source = (blk_index - step_index) % blk_count
        return (visit_pages(state_now, travelling, source * pages_dev), travelling)

    running, travelling = lax.fori_loop(1, blk_count, cycle_step, (running, cache_pages))
    row_max, row_sum, weighted = running
    attended = (
        (weighted / row_sum[..., None])
        .transpose(2, 0, 1, 3)
        .reshape(tok_rows, heads_q * head_dim)
        .astype(jnp.bfloat16)
    )
    full_out = lax.all_gather(out_weight, "blk", axis=1, tiled=True)
    summed = lax.psum_scatter(
        jnp.dot(attended, full_out, preferred_element_type=jnp.float32).astype(jnp.bfloat16),
        "tp",
        scatter_dimension=0,
        tiled=True,
    ).astype(jnp.float32)
    hidden_out = (hidden_f + summed).astype(jnp.bfloat16)
    return (hidden_out, new_pair)


def solution(mesh):
    in_specs = (
        P(("blk", "tp"), None),
        P(),
        P(None, None, "tp"),
        P(None, "tp"),
        P("blk", "tp"),
        P("blk", None, None, "tp", None),
        P("tp", "blk"),
        P(),
        P(),
    )
    out_specs = (P(("blk", "tp"), None), P("blk", None, "tp", None))
    return jax.shard_map(local, mesh=mesh, in_specs=in_specs, out_specs=out_specs, check_vma=False)
```

profile of v0, /device:TPU:1, one launch (start us, length us, event | category | flops | bytes accessed | tf_op | source)
XLA Modules:
  0.0 883.6 jit_solution(6298104520761731236)
XLA Ops:
  18.6 22.0 %all-gather.3.cloned.1.call-done = bf16[128,5120]{1,0:T(8,128)(2,1)} async-done(((bf16[32,5120]{1,0:T(8,128)(2,1)}), bf16[128,5120]{1,0:T(8,128)(2,1)}) %all-gather.3.cloned.1.call-update) | async-done | bytes 1310736 | tf_op jit(solution)/shard_map/all_gather | solution.py:71
  45.6 774.5 %while.45 = (s32[]{:T(128)}, f32[2,5,128]{2,1,0:T(8,128)S(1)}, f32[2,5,128]{2,1,0:T(8,128)S(1)}, f32[2,5,128,128]{3,2,1,0:T(8,128)S(1)}, bf16[1,128,2,2,128]{4,1...) while((s32[]{:T(128)}, f32[2,5,128]{2,1,0:T(8,128)S(1)}, ...), condition=%wide.region_16.17_spmd.clone.clone, body=%wide.region_9.16_spmd.clone.clone.sunk | while | flops 85363664 | bytes 4612620 | solution.py:125
  48.2 9.0 %collective-permute-done = bf16[1,128,2,2,128]{4,1,3,2,0:T(8,128)(2,1)S(1)} collective-permute-done((bf16[1,128,2,2,128]{4,1,3,2,0:T(8,128)(2,1)S(1)}, bf16[1,128,2,2,128]{4,1,3,2,0:T(8,128)(2,1)S(1)}, u32[]{:S(2)}, u32[]{:S(2)}) %collective-permute-start) | collective-permute-done | bytes 131104 | tf_op jit(solution)/shard_map/while/body/eval_jaxpr/ppermute | solution.py:12
  58.6 15.5 %collective-permute-done = bf16[1,128,2,2,128]{4,1,3,2,0:T(8,128)(2,1)S(1)} collective-permute-done((bf16[1,128,2,2,128]{4,1,3,2,0:T(8,128)(2,1)S(1)}, bf16[1,128,2,2,128]{4,1,3,2,0:T(8,128)(2,1)S(1)}, u32[]{:S(2)}, u32[]{:S(2)}) %collective-permute-start) | collective-permute-done | bytes 131104 | tf_op jit(solution)/shard_map/while/body/eval_jaxpr/ppermute | solution.py:12
  75.6 8.8 collective-permute-done
  85.8 14.2 %collective-permute-done = bf16[1,128,2,2,128]{4,1,3,2,0:T(8,128)(2,1)S(1)} collective-permute-done((bf16[1,128,2,2,128]{4,1,3,2,0:T(8,128)(2,1)S(1)}, bf16[1,128,2,2,128]{4,1,3,2,0:T(8,128)(2,1)S(1)}, u32[]{:S(2)}, u32[]{:S(2)}) %collective-permute-start) | collective-permute-done | bytes 131104 | tf_op jit(solution)/shard_map/while/body/eval_jaxpr/ppermute | solution.py:12
  101.4 16.7 %collective-permute-done = bf16[1,128,2,2,128]{4,1,3,2,0:T(8,128)(2,1)S(1)} collective-permute-done((bf16[1,128,2,2,128]{4,1,3,2,0:T(8,128)(2,1)S(1)}, bf16[1,128,2,2,128]{4,1,3,2,0:T(8,128)(2,1)S(1)}, u32[]{:S(2)}, u32[]{:S(2)}) %collective-permute-start) | collective-permute-done | bytes 131104 | tf_op jit(solution)/shard_map/while/body/eval_jaxpr/ppermute | solution.py:12
  119.6 13.0 %collective-permute-done = bf16[1,128,2,2,128]{4,1,3,2,0:T(8,128)(2,1)S(1)} collective-permute-done((bf16[1,128,2,2,128]{4,1,3,2,0:T(8,128)(2,1)S(1)}, bf16[1,128,2,2,128]{4,1,3,2,0:T(8,128)(2,1)S(1)}, u32[]{:S(2)}, u32[]{:S(2)}) %collective-permute-start) | collective-permute-done | bytes 131104 | tf_op jit(solution)/shard_map/while/body/eval_jaxpr/ppermute | solution.py:12
  134.0 15.9 %collective-permute-done = bf16[1,128,2,2,128]{4,1,3,2,0:T(8,128)(2,1)S(1)} collective-permute-done((bf16[1,128,2,2,128]{4,1,3,2,0:T(8,128)(2,1)S(1)}, bf16[1,128,2,2,128]{4,1,3,2,0:T(8,128)(2,1)S(1)}, u32[]{:S(2)}, u32[]{:S(2)}) %collective-permute-start) | collective-permute-done | bytes 131104 | tf_op jit(solution)/shard_map/while/body/eval_jaxpr/ppermute | solution.py:12
  151.4 15.2 %collective-permute-done = bf16[1,128,2,2,128]{4,1,3,2,0:T(8,128)(2,1)S(1)} collective-permute-done((bf16[1,128,2,2,128]{4,1,3,2,0:T(8,128)(2,1)S(1)}, bf16[1,128,2,2,128]{4,1,3,2,0:T(8,128)(2,1)S(1)}, u32[]{:S(2)}, u32[]{:S(2)}) %collective-permute-start) | collective-permute-done | bytes 131104 | tf_op jit(solution)/shard_map/while/body/eval_jaxpr/ppermute | solution.py:12
  168.1 14.3 %collective-permute-done = bf16[1,128,2,2,128]{4,1,3,2,0:T(8,128)(2,1)S(1)} collective-permute-done((bf16[1,128,2,2,128]{4,1,3,2,0:T(8,128)(2,1)S(1)}, bf16[1,128,2,2,128]{4,1,3,2,0:T(8,128)(2,1)S(1)}, u32[]{:S(2)}, u32[]{:S(2)}) %collective-permute-start) | collective-permute-done | bytes 131104 | tf_op jit(solution)/shard_map/while/body/eval_jaxpr/ppermute | solution.py:12
  183.8 14.1 %collective-permute-done = bf16[1,128,2,2,128]{4,1,3,2,0:T(8,128)(2,1)S(1)} collective-permute-done((bf16[1,128,2,2,128]{4,1,3,2,0:T(8,128)(2,1)S(1)}, bf16[1,128,2,2,128]{4,1,3,2,0:T(8,128)(2,1)S(1)}, u32[]{:S(2)}, u32[]{:S(2)}) %collective-permute-start) | collective-permute-done | bytes 131104 | tf_op jit(solution)/shard_map/while/body/eval_jaxpr/ppermute | solution.py:12
  199.3 12.9 %collective-permute-done = bf16[1,128,2,2,128]{4,1,3,2,0:T(8,128)(2,1)S(1)} collective-permute-done((bf16[1,128,2,2,128]{4,1,3,2,0:T(8,128)(2,1)S(1)}, bf16[1,128,2,2,128]{4,1,3,2,0:T(8,128)(2,1)S(1)}, u32[]{:S(2)}, u32[]{:S(2)}) %collective-permute-start) | collective-permute-done | bytes 131104 | tf_op jit(solution)/shard_map/while/body/eval_jaxpr/ppermute | solution.py:12
  213.6 23.3 %collective-permute-done = bf16[1,128,2,2,128]{4,1,3,2,0:T(8,128)(2,1)S(1)} collective-permute-done((bf16[1,128,2,2,128]{4,1,3,2,0:T(8,128)(2,1)S(1)}, bf16[1,128,2,2,128]{4,1,3,2,0:T(8,128)(2,1)S(1)}, u32[]{:S(2)}, u32[]{:S(2)}) %collective-permute-start) | collective-permute-done | bytes 131104 | tf_op jit(solution)/shard_map/while/body/eval_jaxpr/ppermute | solution.py:12
  238.3 11.6 %collective-permute-done = bf16[1,128,2,2,128]{4,1,3,2,0:T(8,128)(2,1)S(1)} collective-permute-done((bf16[1,128,2,2,128]{4,1,3,2,0:T(8,128)(2,1)S(1)}, bf16[1,128,2,2,128]{4,1,3,2,0:T(8,128)(2,1)S(1)}, u32[]{:S(2)}, u32[]{:S(2)}) %collective-permute-start) | collective-permute-done | bytes 131104 | tf_op jit(solution)/shard_map/while/body/eval_jaxpr/ppermute | solution.py:12
  251.4 10.6 %collective-permute-done = bf16[1,128,2,2,128]{4,1,3,2,0:T(8,128)(2,1)S(1)} collective-permute-done((bf16[1,128,2,2,128]{4,1,3,2,0:T(8,128)(2,1)S(1)}, bf16[1,128,2,2,128]{4,1,3,2,0:T(8,128)(2,1)S(1)}, u32[]{:S(2)}, u32[]{:S(2)}) %collective-permute-start) | collective-permute-done | bytes 131104 | tf_op jit(solution)/shard_map/while/body/eval_jaxpr/ppermute | solution.py:12
  283.9 8.9 %collective-permute-done = bf16[1,128,2,2,128]{4,1,3,2,0:T(8,128)(2,1)S(1)} collective-permute-done((bf16[1,128,2,2,128]{4,1,3,2,0:T(8,128)(2,1)S(1)}, bf16[1,128,2,2,128]{4,1,3,2,0:T(8,128)(2,1)S(1)}, u32[]{:S(2)}, u32[]{:S(2)}) %collective-permute-start) | collective-permute-done | bytes 131104 | tf_op jit(solution)/shard_map/while/body/eval_jaxpr/ppermute | solution.py:12
  304.5 8.9 %collective-permute-done = bf16[1,128,2,2,128]{4,1,3,2,0:T(8,128)(2,1)S(1)} collective-permute-done((bf16[1,128,2,2,128]{4,1,3,2,0:T(8,128)(2,1)S(1)}, bf16[1,128,2,2,128]{4,1,3,2,0:T(8,128)(2,1)S(1)}, u32[]{:S(2)}, u32[]{:S(2)}) %collective-permute-start) | collective-permute-done | bytes 131104 | tf_op jit(solution)/shard_map/while/body/eval_jaxpr/ppermute | solution.py:12
  314.8 8.9 %collective-permute-done = bf16[1,128,2,2,128]{4,1,3,2,0:T(8,128)(2,1)S(1)} collective-permute-done((bf16[1,128,2,2,128]{4,1,3,2,0:T(8,128)(2,1)S(1)}, bf16[1,128,2,2,128]{4,1,3,2,0:T(8,128)(2,1)S(1)}, u32[]{:S(2)}, u32[]{:S(2)}) %collective-permute-start) | collective-permute-done | bytes 131104 | tf_op jit(solution)/shard_map/while/body/eval_jaxpr/ppermute | solution.py:12
  325.1 10.7 %collective-permute-done = bf16[1,128,2,2,128]{4,1,3,2,0:T(8,128)(2,1)S(1)} collective-permute-done((bf16[1,128,2,2,128]{4,1,3,2,0:T(8,128)(2,1)S(1)}, bf16[1,128,2,2,128]{4,1,3,2,0:T(8,128)(2,1)S(1)}, u32[]{:S(2)}, u32[]{:S(2)}) %collective-permute-start) | collective-permute-done | bytes 131104 | tf_op jit(solution)/shard_map/while/body/eval_jaxpr/ppermute | solution.py:12
  337.3 9.9 %collective-permute-done = bf16[1,128,2,2,128]{4,1,3,2,0:T(8,128)(2,1)S(1)} collective-permute-done((bf16[1,128,2,2,128]{4,1,3,2,0:T(8,128)(2,1)S(1)}, bf16[1,128,2,2,128]{4,1,3,2,0:T(8,128)(2,1)S(1)}, u32[]{:S(2)}, u32[]{:S(2)}) %collective-permute-start) | collective-permute-done | bytes 131104 | tf_op jit(solution)/shard_map/while/body/eval_jaxpr/ppermute | solution.py:12
  348.7 12.0 %collective-permute-done = bf16[1,128,2,2,128]{4,1,3,2,0:T(8,128)(2,1)S(1)} collective-permute-done((bf16[1,128,2,2,128]{4,1,3,2,0:T(8,128)(2,1)S(1)}, bf16[1,128,2,2,128]{4,1,3,2,0:T(8,128)(2,1)S(1)}, u32[]{:S(2)}, u32[]{:S(2)}) %collective-permute-start) | collective-permute-done | bytes 131104 | tf_op jit(solution)/shard_map/while/body/eval_jaxpr/ppermute | solution.py:12
  362.1 9.5 %collective-permute-done = bf16[1,128,2,2,128]{4,1,3,2,0:T(8,128)(2,1)S(1)} collective-permute-done((bf16[1,128,2,2,128]{4,1,3,2,0:T(8,128)(2,1)S(1)}, bf16[1,128,2,2,128]{4,1,3,2,0:T(8,128)(2,1)S(1)}, u32[]{:S(2)}, u32[]{:S(2)}) %collective-permute-start) | collective-permute-done | bytes 131104 | tf_op jit(solution)/shard_map/while/body/eval_jaxpr/ppermute | solution.py:12
  373.0 10.2 %collective-permute-done = bf16[1,128,2,2,128]{4,1,3,2,0:T(8,128)(2,1)S(1)} collective-permute-done((bf16[1,128,2,2,128]{4,1,3,2,0:T(8,128)(2,1)S(1)}, bf16[1,128,2,2,128]{4,1,3,2,0:T(8,128)(2,1)S(1)}, u32[]{:S(2)}, u32[]{:S(2)}) %collective-permute-start) | collective-permute-done | bytes 131104 | tf_op jit(solution)/shard_map/while/body/eval_jaxpr/ppermute | solution.py:12
  384.7 8.9 %collective-permute-done = bf16[1,128,2,2,128]{4,1,3,2,0:T(8,128)(2,1)S(1)} collective-permute-done((bf16[1,128,2,2,128]{4,1,3,2,0:T(8,128)(2,1)S(1)}, bf16[1,128,2,2,128]{4,1,3,2,0:T(8,128)(2,1)S(1)}, u32[]{:S(2)}, u32[]{:S(2)}) %collective-permute-start) | collective-permute-done | bytes 131104 | tf_op jit(solution)/shard_map/while/body/eval_jaxpr/ppermute | solution.py:12
  395.1 10.2 %collective-permute-done = bf16[1,128,2,2,128]{4,1,3,2,0:T(8,128)(2,1)S(1)} collective-permute-done((bf16[1,128,2,2,128]{4,1,3,2,0:T(8,128)(2,1)S(1)}, bf16[1,128,2,2,128]{4,1,3,2,0:T(8,128)(2,1)S(1)}, u32[]{:S(2)}, u32[]{:S(2)}) %collective-permute-start) | collective-permute-done | bytes 131104 | tf_op jit(solution)/shard_map/while/body/eval_jaxpr/ppermute | solution.py:12
  406.7 10.2 %collective-permute-done = bf16[1,128,2,2,128]{4,1,3,2,0:T(8,128)(2,1)S(1)} collective-permute-done((bf16[1,128,2,2,128]{4,1,3,2,0:T(8,128)(2,1)S(1)}, bf16[1,128,2,2,128]{4,1,3,2,0:T(8,128)(2,1)S(1)}, u32[]{:S(2)}, u32[]{:S(2)}) %collective-permute-start) | collective-permute-done | bytes 131104 | tf_op jit(solution)/shard_map/while/body/eval_jaxpr/ppermute | solution.py:12
  418.4 10.2 %collective-permute-done = bf16[1,128,2,2,128]{4,1,3,2,0:T(8,128)(2,1)S(1)} collective-permute-done((bf16[1,128,2,2,128]{4,1,3,2,0:T(8,128)(2,1)S(1)}, bf16[1,128,2,2,128]{4,1,3,2,0:T(8,128)(2,1)S(1)}, u32[]{:S(2)}, u32[]{:S(2)}) %collective-permute-start) | collective-permute-done | bytes 131104 | tf_op jit(solution)/shard_map/while/body/eval_jaxpr/ppermute | solution.py:12
  430.0 10.2 %collective-permute-done = bf16[1,128,2,2,128]{4,1,3,2,0:T(8,128)(2,1)S(1)} collective-permute-done((bf16[1,128,2,2,128]{4,1,3,2,0:T(8,128)(2,1)S(1)}, bf16[1,128,2,2,128]{4,1,3,2,0:T(8,128)(2,1)S(1)}, u32[]{:S(2)}, u32[]{:S(2)}) %collective-permute-start) | collective-permute-done | bytes 131104 | tf_op jit(solution)/shard_map/while/body/eval_jaxpr/ppermute | solution.py:12
  441.7 10.1 %collective-permute-done = bf16[1,128,2,2,128]{4,1,3,2,0:T(8,128)(2,1)S(1)} collective-permute-done((bf16[1,128,2,2,128]{4,1,3,2,0:T(8,128)(2,1)S(1)}, bf16[1,128,2,2,128]{4,1,3,2,0:T(8,128)(2,1)S(1)}, u32[]{:S(2)}, u32[]{:S(2)}) %collective-permute-start) | collective-permute-done | bytes 131104 | tf_op jit(solution)/shard_map/while/body/eval_jaxpr/ppermute | solution.py:12
  453.2 10.2 %collective-permute-done = bf16[1,128,2,2,128]{4,1,3,2,0:T(8,128)(2,1)S(1)} collective-permute-done((bf16[1,128,2,2,128]{4,1,3,2,0:T(8,128)(2,1)S(1)}, bf16[1,128,2,2,128]{4,1,3,2,0:T(8,128)(2,1)S(1)}, u32[]{:S(2)}, u32[]{:S(2)}) %collective-permute-start) | collective-permute-done | bytes 131104 | tf_op jit(solution)/shard_map/while/body/eval_jaxpr/ppermute | solution.py:12
  464.9 10.2 %collective-permute-done = bf16[1,128,2,2,128]{4,1,3,2,0:T(8,128)(2,1)S(1)} collective-permute-done((bf16[1,128,2,2,128]{4,1,3,2,0:T(8,128)(2,1)S(1)}, bf16[1,128,2,2,128]{4,1,3,2,0:T(8,128)(2,1)S(1)}, u32[]{:S(2)}, u32[]{:S(2)}) %collective-permute-start) | collective-permute-done | bytes 131104 | tf_op jit(solution)/shard_map/while/body/eval_jaxpr/ppermute | solution.py:12
  476.5 9.8 %collective-permute-done = bf16[1,128,2,2,128]{4,1,3,2,0:T(8,128)(2,1)S(1)} collective-permute-done((bf16[1,128,2,2,128]{4,1,3,2,0:T(8,128)(2,1)S(1)}, bf16[1,128,2,2,128]{4,1,3,2,0:T(8,128)(2,1)S(1)}, u32[]{:S(2)}, u32[]{:S(2)}) %collective-permute-start) | collective-permute-done | bytes 131104 | tf_op jit(solution)/shard_map/while/body/eval_jaxpr/ppermute | solution.py:12
  487.8 10.2 %collective-permute-done = bf16[1,128,2,2,128]{4,1,3,2,0:T(8,128)(2,1)S(1)} collective-permute-done((bf16[1,128,2,2,128]{4,1,3,2,0:T(8,128)(2,1)S(1)}, bf16[1,128,2,2,128]{4,1,3,2,0:T(8,128)(2,1)S(1)}, u32[]{:S(2)}, u32[]{:S(2)}) %collective-permute-start) | collective-permute-done | bytes 131104 | tf_op jit(solution)/shard_map/while/body/eval_jaxpr/ppermute | solution.py:12
  499.4 9.9 %collective-permute-done = bf16[1,128,2,2,128]{4,1,3,2,0:T(8,128)(2,1)S(1)} collective-permute-done((bf16[1,128,2,2,128]{4,1,3,2,0:T(8,128)(2,1)S(1)}, bf16[1,128,2,2,128]{4,1,3,2,0:T(8,128)(2,1)S(1)}, u32[]{:S(2)}, u32[]{:S(2)}) %collective-permute-start) | collective-permute-done | bytes 131104 | tf_op jit(solution)/shard_map/while/body/eval_jaxpr/ppermute | solution.py:12
  510.8 10.1 %collective-permute-done = bf16[1,128,2,2,128]{4,1,3,2,0:T(8,128)(2,1)S(1)} collective-permute-done((bf16[1,128,2,2,128]{4,1,3,2,0:T(8,128)(2,1)S(1)}, bf16[1,128,2,2,128]{4,1,3,2,0:T(8,128)(2,1)S(1)}, u32[]{:S(2)}, u32[]{:S(2)}) %collective-permute-start) | collective-permute-done | bytes 131104 | tf_op jit(solution)/shard_map/while/body/eval_jaxpr/ppermute | solution.py:12
  522.3 10.2 %collective-permute-done = bf16[1,128,2,2,128]{4,1,3,2,0:T(8,128)(2,1)S(1)} collective-permute-done((bf16[1,128,2,2,128]{4,1,3,2,0:T(8,128)(2,1)S(1)}, bf16[1,128,2,2,128]{4,1,3,2,0:T(8,128)(2,1)S(1)}, u32[]{:S(2)}, u32[]{:S(2)}) %collective-permute-start) | collective-permute-done | bytes 131104 | tf_op jit(solution)/shard_map/while/body/eval_jaxpr/ppermute | solution.py:12
  533.9 10.2 %collective-permute-done = bf16[1,128,2,2,128]{4,1,3,2,0:T(8,128)(2,1)S(1)} collective-permute-done((bf16[1,128,2,2,128]{4,1,3,2,0:T(8,128)(2,1)S(1)}, bf16[1,128,2,2,128]{4,1,3,2,0:T(8,128)(2,1)S(1)}, u32[]{:S(2)}, u32[]{:S(2)}) %collective-permute-start) | collective-permute-done | bytes 131104 | tf_op jit(solution)/shard_map/while/body/eval_jaxpr/ppermute | solution.py:12
  545.6 10.2 %collective-permute-done = bf16[1,128,2,2,128]{4,1,3,2,0:T(8,128)(2,1)S(1)} collective-permute-done((bf16[1,128,2,2,128]{4,1,3,2,0:T(8,128)(2,1)S(1)}, bf16[1,128,2,2,128]{4,1,3,2,0:T(8,128)(2,1)S(1)}, u32[]{:S(2)}, u32[]{:S(2)}) %collective-permute-start) | collective-permute-done | bytes 131104 | tf_op jit(solution)/shard_map/while/body/eval_jaxpr/ppermute | solution.py:12
  557.2 10.5 %collective-permute-done = bf16[1,128,2,2,128]{4,1,3,2,0:T(8,128)(2,1)S(1)} collective-permute-done((bf16[1,128,2,2,128]{4,1,3,2,0:T(8,128)(2,1)S(1)}, bf16[1,128,2,2,128]{4,1,3,2,0:T(8,128)(2,1)S(1)}, u32[]{:S(2)}, u32[]{:S(2)}) %collective-permute-start) | collective-permute-done | bytes 131104 | tf_op jit(solution)/shard_map/while/body/eval_jaxpr/ppermute | solution.py:12
  569.1 9.3 %collective-permute-done = bf16[1,128,2,2,128]{4,1,3,2,0:T(8,128)(2,1)S(1)} collective-permute-done((bf16[1,128,2,2,128]{4,1,3,2,0:T(8,128)(2,1)S(1)}, bf16[1,128,2,2,128]{4,1,3,2,0:T(8,128)(2,1)S(1)}, u32[]{:S(2)}, u32[]{:S(2)}) %collective-permute-start) | collective-permute-done | bytes 131104 | tf_op jit(solution)/shard_map/while/body/eval_jaxpr/ppermute | solution.py:12
  579.8 10.1 %collective-permute-done = bf16[1,128,2,2,128]{4,1,3,2,0:T(8,128)(2,1)S(1)} collective-permute-done((bf16[1,128,2,2,128]{4,1,3,2,0:T(8,128)(2,1)S(1)}, bf16[1,128,2,2,128]{4,1,3,2,0:T(8,128)(2,1)S(1)}, u32[]{:S(2)}, u32[]{:S(2)}) %collective-permute-start) | collective-permute-done | bytes 131104 | tf_op jit(solution)/shard_map/while/body/eval_jaxpr/ppermute | solution.py:12
  591.4 10.2 %collective-permute-done = bf16[1,128,2,2,128]{4,1,3,2,0:T(8,128)(2,1)S(1)} collective-permute-done((bf16[1,128,2,2,128]{4,1,3,2,0:T(8,128)(2,1)S(1)}, bf16[1,128,2,2,128]{4,1,3,2,0:T(8,128)(2,1)S(1)}, u32[]{:S(2)}, u32[]{:S(2)}) %collective-permute-start) | collective-permute-done | bytes 131104 | tf_op jit(solution)/shard_map/while/body/eval_jaxpr/ppermute | solution.py:12
  603.0 10.0 %collective-permute-done = bf16[1,128,2,2,128]{4,1,3,2,0:T(8,128)(2,1)S(1)} collective-permute-done((bf16[1,128,2,2,128]{4,1,3,2,0:T(8,128)(2,1)S(1)}, bf16[1,128,2,2,128]{4,1,3,2,0:T(8,128)(2,1)S(1)}, u32[]{:S(2)}, u32[]{:S(2)}) %collective-permute-start) | collective-permute-done | bytes 131104 | tf_op jit(solution)/shard_map/while/body/eval_jaxpr/ppermute | solution.py:12
  614.4 10.1 %collective-permute-done = bf16[1,128,2,2,128]{4,1,3,2,0:T(8,128)(2,1)S(1)} collective-permute-done((bf16[1,128,2,2,128]{4,1,3,2,0:T(8,128)(2,1)S(1)}, bf16[1,128,2,2,128]{4,1,3,2,0:T(8,128)(2,1)S(1)}, u32[]{:S(2)}, u32[]{:S(2)}) %collective-permute-start) | collective-permute-done | bytes 131104 | tf_op jit(solution)/shard_map/while/body/eval_jaxpr/ppermute | solution.py:12
  626.0 10.1 %collective-permute-done = bf16[1,128,2,2,128]{4,1,3,2,0:T(8,128)(2,1)S(1)} collective-permute-done((bf16[1,128,2,2,128]{4,1,3,2,0:T(8,128)(2,1)S(1)}, bf16[1,128,2,2,128]{4,1,3,2,0:T(8,128)(2,1)S(1)}, u32[]{:S(2)}, u32[]{:S(2)}) %collective-permute-start) | collective-permute-done | bytes 131104 | tf_op jit(solution)/shard_map/while/body/eval_jaxpr/ppermute | solution.py:12
  637.5 10.2 %collective-permute-done = bf16[1,128,2,2,128]{4,1,3,2,0:T(8,128)(2,1)S(1)} collective-permute-done((bf16[1,128,2,2,128]{4,1,3,2,0:T(8,128)(2,1)S(1)}, bf16[1,128,2,2,128]{4,1,3,2,0:T(8,128)(2,1)S(1)}, u32[]{:S(2)}, u32[]{:S(2)}) %collective-permute-start) | collective-permute-done | bytes 131104 | tf_op jit(solution)/shard_map/while/body/eval_jaxpr/ppermute | solution.py:12
  649.1 9.9 %collective-permute-done = bf16[1,128,2,2,128]{4,1,3,2,0:T(8,128)(2,1)S(1)} collective-permute-done((bf16[1,128,2,2,128]{4,1,3,2,0:T(8,128)(2,1)S(1)}, bf16[1,128,2,2,128]{4,1,3,2,0:T(8,128)(2,1)S(1)}, u32[]{:S(2)}, u32[]{:S(2)}) %collective-permute-start) | collective-permute-done | bytes 131104 | tf_op jit(solution)/shard_map/while/body/eval_jaxpr/ppermute | solution.py:12
  660.5 10.1 %collective-permute-done = bf16[1,128,2,2,128]{4,1,3,2,0:T(8,128)(2,1)S(1)} collective-permute-done((bf16[1,128,2,2,128]{4,1,3,2,0:T(8,128)(2,1)S(1)}, bf16[1,128,2,2,128]{4,1,3,2,0:T(8,128)(2,1)S(1)}, u32[]{:S(2)}, u32[]{:S(2)}) %collective-permute-start) | collective-permute-done | bytes 131104 | tf_op jit(solution)/shard_map/while/body/eval_jaxpr/ppermute | solution.py:12
  672.0 10.1 %collective-permute-done = bf16[1,128,2,2,128]{4,1,3,2,0:T(8,128)(2,1)S(1)} collective-permute-done((bf16[1,128,2,2,128]{4,1,3,2,0:T(8,128)(2,1)S(1)}, bf16[1,128,2,2,128]{4,1,3,2,0:T(8,128)(2,1)S(1)}, u32[]{:S(2)}, u32[]{:S(2)}) %collective-permute-start) | collective-permute-done | bytes 131104 | tf_op jit(solution)/shard_map/while/body/eval_jaxpr/ppermute | solution.py:12
  683.5 10.1 %collective-permute-done = bf16[1,128,2,2,128]{4,1,3,2,0:T(8,128)(2,1)S(1)} collective-permute-done((bf16[1,128,2,2,128]{4,1,3,2,0:T(8,128)(2,1)S(1)}, bf16[1,128,2,2,128]{4,1,3,2,0:T(8,128)(2,1)S(1)}, u32[]{:S(2)}, u32[]{:S(2)}) %collective-permute-start) | collective-permute-done | bytes 131104 | tf_op jit(solution)/shard_map/while/body/eval_jaxpr/ppermute | solution.py:12
  695.0 10.1 %collective-permute-done = bf16[1,128,2,2,128]{4,1,3,2,0:T(8,128)(2,1)S(1)} collective-permute-done((bf16[1,128,2,2,128]{4,1,3,2,0:T(8,128)(2,1)S(1)}, bf16[1,128,2,2,128]{4,1,3,2,0:T(8,128)(2,1)S(1)}, u32[]{:S(2)}, u32[]{:S(2)}) %collective-permute-start) | collective-permute-done | bytes 131104 | tf_op jit(solution)/shard_map/while/body/eval_jaxpr/ppermute | solution.py:12
  706.5 10.1 %collective-permute-done = bf16[1,128,2,2,128]{4,1,3,2,0:T(8,128)(2,1)S(1)} collective-permute-done((bf16[1,128,2,2,128]{4,1,3,2,0:T(8,128)(2,1)S(1)}, bf16[1,128,2,2,128]{4,1,3,2,0:T(8,128)(2,1)S(1)}, u32[]{:S(2)}, u32[]{:S(2)}) %collective-permute-start) | collective-permute-done | bytes 131104 | tf_op jit(solution)/shard_map/while/body/eval_jaxpr/ppermute | solution.py:12
  718.0 10.2 %collective-permute-done = bf16[1,128,2,2,128]{4,1,3,2,0:T(8,128)(2,1)S(1)} collective-permute-done((bf16[1,128,2,2,128]{4,1,3,2,0:T(8,128)(2,1)S(1)}, bf16[1,128,2,2,128]{4,1,3,2,0:T(8,128)(2,1)S(1)}, u32[]{:S(2)}, u32[]{:S(2)}) %collective-permute-start) | collective-permute-done | bytes 131104 | tf_op jit(solution)/shard_map/while/body/eval_jaxpr/ppermute | solution.py:12
  729.7 9.9 %collective-permute-done = bf16[1,128,2,2,128]{4,1,3,2,0:T(8,128)(2,1)S(1)} collective-permute-done((bf16[1,128,2,2,128]{4,1,3,2,0:T(8,128)(2,1)S(1)}, bf16[1,128,2,2,128]{4,1,3,2,0:T(8,128)(2,1)S(1)}, u32[]{:S(2)}, u32[]{:S(2)}) %collective-permute-start) | collective-permute-done | bytes 131104 | tf_op jit(solution)/shard_map/while/body/eval_jaxpr/ppermute | solution.py:12
  741.0 10.2 %collective-permute-done = bf16[1,128,2,2,128]{4,1,3,2,0:T(8,128)(2,1)S(1)} collective-permute-done((bf16[1,128,2,2,128]{4,1,3,2,0:T(8,128)(2,1)S(1)}, bf16[1,128,2,2,128]{4,1,3,2,0:T(8,128)(2,1)S(1)}, u32[]{:S(2)}, u32[]{:S(2)}) %collective-permute-start) | collective-permute-done | bytes 131104 | tf_op jit(solution)/shard_map/while/body/eval_jaxpr/ppermute | solution.py:12
  752.7 10.2 %collective-permute-done = bf16[1,128,2,2,128]{4,1,3,2,0:T(8,128)(2,1)S(1)} collective-permute-done((bf16[1,128,2,2,128]{4,1,3,2,0:T(8,128)(2,1)S(1)}, bf16[1,128,2,2,128]{4,1,3,2,0:T(8,128)(2,1)S(1)}, u32[]{:S(2)}, u32[]{:S(2)}) %collective-permute-start) | collective-permute-done | bytes 131104 | tf_op jit(solution)/shard_map/while/body/eval_jaxpr/ppermute | solution.py:12
  764.3 9.8 %collective-permute-done = bf16[1,128,2,2,128]{4,1,3,2,0:T(8,128)(2,1)S(1)} collective-permute-done((bf16[1,128,2,2,128]{4,1,3,2,0:T(8,128)(2,1)S(1)}, bf16[1,128,2,2,128]{4,1,3,2,0:T(8,128)(2,1)S(1)}, u32[]{:S(2)}, u32[]{:S(2)}) %collective-permute-start) | collective-permute-done | bytes 131104 | tf_op jit(solution)/shard_map/while/body/eval_jaxpr/ppermute | solution.py:12
  775.5 10.1 %collective-permute-done = bf16[1,128,2,2,128]{4,1,3,2,0:T(8,128)(2,1)S(1)} collective-permute-done((bf16[1,128,2,2,128]{4,1,3,2,0:T(8,128)(2,1)S(1)}, bf16[1,128,2,2,128]{4,1,3,2,0:T(8,128)(2,1)S(1)}, u32[]{:S(2)}, u32[]{:S(2)}) %collective-permute-start) | collective-permute-done | bytes 131104 | tf_op jit(solution)/shard_map/while/body/eval_jaxpr/ppermute | solution.py:12
  787.0 10.1 %collective-permute-done = bf16[1,128,2,2,128]{4,1,3,2,0:T(8,128)(2,1)S(1)} collective-permute-done((bf16[1,128,2,2,128]{4,1,3,2,0:T(8,128)(2,1)S(1)}, bf16[1,128,2,2,128]{4,1,3,2,0:T(8,128)(2,1)S(1)}, u32[]{:S(2)}, u32[]{:S(2)}) %collective-permute-start) | collective-permute-done | bytes 131104 | tf_op jit(solution)/shard_map/while/body/eval_jaxpr/ppermute | solution.py:12
  798.5 10.1 %collective-permute-done = bf16[1,128,2,2,128]{4,1,3,2,0:T(8,128)(2,1)S(1)} collective-permute-done((bf16[1,128,2,2,128]{4,1,3,2,0:T(8,128)(2,1)S(1)}, bf16[1,128,2,2,128]{4,1,3,2,0:T(8,128)(2,1)S(1)}, u32[]{:S(2)}, u32[]{:S(2)}) %collective-permute-start) | collective-permute-done | bytes 131104 | tf_op jit(solution)/shard_map/while/body/eval_jaxpr/ppermute | solution.py:12
  810.0 10.1 %collective-permute-done = bf16[1,128,2,2,128]{4,1,3,2,0:T(8,128)(2,1)S(1)} collective-permute-done((bf16[1,128,2,2,128]{4,1,3,2,0:T(8,128)(2,1)S(1)}, bf16[1,128,2,2,128]{4,1,3,2,0:T(8,128)(2,1)S(1)}, u32[]{:S(2)}, u32[]{:S(2)}) %collective-permute-start) | collective-permute-done | bytes 131104 | tf_op jit(solution)/shard_map/while/body/eval_jaxpr/ppermute | solution.py:12
  820.5 10.3 %convolution_convert_fusion = bf16[128,5120]{1,0:T(8,128)(2,1)} fusion(bf16[128,1280]{0,1:T(8,128)(2,1)S(1)} %bitcast.85, bf16[1280,5120]{0,1:T(8,128)(2,1)} %all-gather.5.cloned.1.call-done), kind=kOutput, calls=%fused_computation.32 | convolution fusion | flops 1678376960 | bytes 14745600 | tf_op jit(solution)/shard_map/dot_general | solution.py:135
  831.7 43.5 %reduce-scatter.2.cloned.1.call-done = bf16[32,5120]{1,0:T(8,128)(2,1)} async-done(((bf16[128,5120]{1,0:T(8,128)(2,1)}), bf16[32,5120]{1,0:T(8,128)(2,1)}) %reduce-scatter.2.cloned.1.call-update) | async-done | bytes 327696 | tf_op jit(solution)/shard_map/reduce_scatter | solution.py:134
  (437 shorter events, 91.6 us)
Async XLA Ops:
  7.2 33.5 %all-gather.3.cloned.1.call-start = ((), (), s32[]{:S(2)}) async-start(), calls=%async_computation.1 | async-start | bytes 1638400 | tf_op jit(solution)/shard_map/all_gather | solution.py:71
  11.0 809.5 %all-gather.5.cloned.1.call-start = ((), (), s32[]{:S(2)}) async-start(), calls=%async_computation.2 | async-start | bytes 13312000 | tf_op jit(solution)/shard_map/all_gather | solution.py:133
  11.8 863.5 %reduce-scatter.2.cloned.1.call-start = ((), (), s32[]{:S(2)}) async-start(), calls=%async_computation.3 | async-start | bytes 1638400 | tf_op jit(solution)/shard_map/reduce_scatter | solution.py:134
  45.6 11.5 %collective-permute-start = (bf16[1,128,2,2,128]{4,1,3,2,0:T(8,128)(2,1)S(1)}, bf16[1,128,2,2,128]{4,1,3,2,0:T(8,128)(2,1)S(1)}, u32[]{:S(2)}, u32[]{:S(2)}) collective-permute-start(bf16[1,128,2,2,128]{4,1,3,2,0:T(8,128)(2,1)S(1)} %get-tuple-element.798), channel_id=1, source_target_pairs={{0,4},{4,8},{8,12},{12,16},{16,20},{20,24},{24,28},{28,32},{32,36}... | collective-permute-start | bytes 393224 | tf_op jit(solution)/shard_map/while/body/eval_jaxpr/ppermute | solution.py:12
  57.2 16.9 %collective-permute-start = (bf16[1,128,2,2,128]{4,1,3,2,0:T(8,128)(2,1)S(1)}, bf16[1,128,2,2,128]{4,1,3,2,0:T(8,128)(2,1)S(1)}, u32[]{:S(2)}, u32[]{:S(2)}) collective-permute-start(bf16[1,128,2,2,128]{4,1,3,2,0:T(8,128)(2,1)S(1)} %get-tuple-element.798), channel_id=1, source_target_pairs={{0,4},{4,8},{8,12},{12,16},{16,20},{20,24},{24,28},{28,32},{32,36}... | collective-permute-start | bytes 393224 | tf_op jit(solution)/shard_map/while/body/eval_jaxpr/ppermute | solution.py:12
  74.2 10.2 %collective-permute-start = (bf16[1,128,2,2,128]{4,1,3,2,0:T(8,128)(2,1)S(1)}, bf16[1,128,2,2,128]{4,1,3,2,0:T(8,128)(2,1)S(1)}, u32[]{:S(2)}, u32[]{:S(2)}) collective-permute-start(bf16[1,128,2,2,128]{4,1,3,2,0:T(8,128)(2,1)S(1)} %get-tuple-element.798), channel_id=1, source_target_pairs={{0,4},{4,8},{8,12},{12,16},{16,20},{20,24},{24,28},{28,32},{32,36}... | collective-permute-start | bytes 393224 | tf_op jit(solution)/shard_map/while/body/eval_jaxpr/ppermute | solution.py:12
  84.4 15.6 %collective-permute-start = (bf16[1,128,2,2,128]{4,1,3,2,0:T(8,128)(2,1)S(1)}, bf16[1,128,2,2,128]{4,1,3,2,0:T(8,128)(2,1)S(1)}, u32[]{:S(2)}, u32[]{:S(2)}) collective-permute-start(bf16[1,128,2,2,128]{4,1,3,2,0:T(8,128)(2,1)S(1)} %get-tuple-element.798), channel_id=1, source_target_pairs={{0,4},{4,8},{8,12},{12,16},{16,20},{20,24},{24,28},{28,32},{32,36}... | collective-permute-start | bytes 393224 | tf_op jit(solution)/shard_map/while/body/eval_jaxpr/ppermute | solution.py:12
  100.0 18.1 %collective-permute-start = (bf16[1,128,2,2,128]{4,1,3,2,0:T(8,128)(2,1)S(1)}, bf16[1,128,2,2,128]{4,1,3,2,0:T(8,128)(2,1)S(1)}, u32[]{:S(2)}, u32[]{:S(2)}) collective-permute-start(bf16[1,128,2,2,128]{4,1,3,2,0:T(8,128)(2,1)S(1)} %get-tuple-element.798), channel_id=1, source_target_pairs={{0,4},{4,8},{8,12},{12,16},{16,20},{20,24},{24,28},{28,32},{32,36}... | collective-permute-start | bytes 393224 | tf_op jit(solution)/shard_map/while/body/eval_jaxpr/ppermute | solution.py:12
  118.2 14.4 %collective-permute-start = (bf16[1,128,2,2,128]{4,1,3,2,0:T(8,128)(2,1)S(1)}, bf16[1,128,2,2,128]{4,1,3,2,0:T(8,128)(2,1)S(1)}, u32[]{:S(2)}, u32[]{:S(2)}) collective-permute-start(bf16[1,128,2,2,128]{4,1,3,2,0:T(8,128)(2,1)S(1)} %get-tuple-element.798), channel_id=1, source_target_pairs={{0,4},{4,8},{8,12},{12,16},{16,20},{20,24},{24,28},{28,32},{32,36}... | collective-permute-start | bytes 393224 | tf_op jit(solution)/shard_map/while/body/eval_jaxpr/ppermute | solution.py:12
  132.6 17.3 %collective-permute-start = (bf16[1,128,2,2,128]{4,1,3,2,0:T(8,128)(2,1)S(1)}, bf16[1,128,2,2,128]{4,1,3,2,0:T(8,128)(2,1)S(1)}, u32[]{:S(2)}, u32[]{:S(2)}) collective-permute-start(bf16[1,128,2,2,128]{4,1,3,2,0:T(8,128)(2,1)S(1)} %get-tuple-element.798), channel_id=1, source_target_pairs={{0,4},{4,8},{8,12},{12,16},{16,20},{20,24},{24,28},{28,32},{32,36}... | collective-permute-start | bytes 393224 | tf_op jit(solution)/shard_map/while/body/eval_jaxpr/ppermute | solution.py:12
  150.0 16.6 %collective-permute-start = (bf16[1,128,2,2,128]{4,1,3,2,0:T(8,128)(2,1)S(1)}, bf16[1,128,2,2,128]{4,1,3,2,0:T(8,128)(2,1)S(1)}, u32[]{:S(2)}, u32[]{:S(2)}) collective-permute-start(bf16[1,128,2,2,128]{4,1,3,2,0:T(8,128)(2,1)S(1)} %get-tuple-element.798), channel_id=1, source_target_pairs={{0,4},{4,8},{8,12},{12,16},{16,20},{20,24},{24,28},{28,32},{32,36}... | collective-permute-start | bytes 393224 | tf_op jit(solution)/shard_map/while/body/eval_jaxpr/ppermute | solution.py:12
  166.7 15.7 %collective-permute-start = (bf16[1,128,2,2,128]{4,1,3,2,0:T(8,128)(2,1)S(1)}, bf16[1,128,2,2,128]{4,1,3,2,0:T(8,128)(2,1)S(1)}, u32[]{:S(2)}, u32[]{:S(2)}) collective-permute-start(bf16[1,128,2,2,128]{4,1,3,2,0:T(8,128)(2,1)S(1)} %get-tuple-element.798), channel_id=1, source_target_pairs={{0,4},{4,8},{8,12},{12,16},{16,20},{20,24},{24,28},{28,32},{32,36}... | collective-permute-start | bytes 393224 | tf_op jit(solution)/shard_map/while/body/eval_jaxpr/ppermute | solution.py:12
  182.4 15.5 %collective-permute-start = (bf16[1,128,2,2,128]{4,1,3,2,0:T(8,128)(2,1)S(1)}, bf16[1,128,2,2,128]{4,1,3,2,0:T(8,128)(2,1)S(1)}, u32[]{:S(2)}, u32[]{:S(2)}) collective-permute-start(bf16[1,128,2,2,128]{4,1,3,2,0:T(8,128)(2,1)S(1)} %get-tuple-element.798), channel_id=1, source_target_pairs={{0,4},{4,8},{8,12},{12,16},{16,20},{20,24},{24,28},{28,32},{32,36}... | collective-permute-start | bytes 393224 | tf_op jit(solution)/shard_map/while/body/eval_jaxpr/ppermute | solution.py:12
  197.9 14.3 %collective-permute-start = (bf16[1,128,2,2,128]{4,1,3,2,0:T(8,128)(2,1)S(1)}, bf16[1,128,2,2,128]{4,1,3,2,0:T(8,128)(2,1)S(1)}, u32[]{:S(2)}, u32[]{:S(2)}) collective-permute-start(bf16[1,128,2,2,128]{4,1,3,2,0:T(8,128)(2,1)S(1)} %get-tuple-element.798), channel_id=1, source_target_pairs={{0,4},{4,8},{8,12},{12,16},{16,20},{20,24},{24,28},{28,32},{32,36}... | collective-permute-start | bytes 393224 | tf_op jit(solution)/shard_map/while/body/eval_jaxpr/ppermute | solution.py:12
  212.2 24.7 %collective-permute-start = (bf16[1,128,2,2,128]{4,1,3,2,0:T(8,128)(2,1)S(1)}, bf16[1,128,2,2,128]{4,1,3,2,0:T(8,128)(2,1)S(1)}, u32[]{:S(2)}, u32[]{:S(2)}) collective-permute-start(bf16[1,128,2,2,128]{4,1,3,2,0:T(8,128)(2,1)S(1)} %get-tuple-element.798), channel_id=1, source_target_pairs={{0,4},{4,8},{8,12},{12,16},{16,20},{20,24},{24,28},{28,32},{32,36}... | collective-permute-start | bytes 393224 | tf_op jit(solution)/shard_map/while/body/eval_jaxpr/ppermute | solution.py:12
  236.9 13.0 %collective-permute-start = (bf16[1,128,2,2,128]{4,1,3,2,0:T(8,128)(2,1)S(1)}, bf16[1,128,2,2,128]{4,1,3,2,0:T(8,128)(2,1)S(1)}, u32[]{:S(2)}, u32[]{:S(2)}) collective-permute-start(bf16[1,128,2,2,128]{4,1,3,2,0:T(8,128)(2,1)S(1)} %get-tuple-element.798), channel_id=1, source_target_pairs={{0,4},{4,8},{8,12},{12,16},{16,20},{20,24},{24,28},{28,32},{32,36}... | collective-permute-start | bytes 393224 | tf_op jit(solution)/shard_map/while/body/eval_jaxpr/ppermute | solution.py:12
  250.0 12.0 %collective-permute-start = (bf16[1,128,2,2,128]{4,1,3,2,0:T(8,128)(2,1)S(1)}, bf16[1,128,2,2,128]{4,1,3,2,0:T(8,128)(2,1)S(1)}, u32[]{:S(2)}, u32[]{:S(2)}) collective-permute-start(bf16[1,128,2,2,128]{4,1,3,2,0:T(8,128)(2,1)S(1)} %get-tuple-element.798), channel_id=1, source_target_pairs={{0,4},{4,8},{8,12},{12,16},{16,20},{20,24},{24,28},{28,32},{32,36}... | collective-permute-start | bytes 393224 | tf_op jit(solution)/shard_map/while/body/eval_jaxpr/ppermute | solution.py:12
  272.2 10.2 %collective-permute-start = (bf16[1,128,2,2,128]{4,1,3,2,0:T(8,128)(2,1)S(1)}, bf16[1,128,2,2,128]{4,1,3,2,0:T(8,128)(2,1)S(1)}, u32[]{:S(2)}, u32[]{:S(2)}) collective-permute-start(bf16[1,128,2,2,128]{4,1,3,2,0:T(8,128)(2,1)S(1)} %get-tuple-element.798), channel_id=1, source_target_pairs={{0,4},{4,8},{8,12},{12,16},{16,20},{20,24},{24,28},{28,32},{32,36}... | collective-permute-start | bytes 393224 | tf_op jit(solution)/shard_map/while/body/eval_jaxpr/ppermute | solution.py:12
  282.5 10.3 %collective-permute-start = (bf16[1,128,2,2,128]{4,1,3,2,0:T(8,128)(2,1)S(1)}, bf16[1,128,2,2,128]{4,1,3,2,0:T(8,128)(2,1)S(1)}, u32[]{:S(2)}, u32[]{:S(2)}) collective-permute-start(bf16[1,128,2,2,128]{4,1,3,2,0:T(8,128)(2,1)S(1)} %get-tuple-element.798), channel_id=1, source_target_pairs={{0,4},{4,8},{8,12},{12,16},{16,20},{20,24},{24,28},{28,32},{32,36}... | collective-permute-start | bytes 393224 | tf_op jit(solution)/shard_map/while/body/eval_jaxpr/ppermute | solution.py:12
  303.1 10.3 %collective-permute-start = (bf16[1,128,2,2,128]{4,1,3,2,0:T(8,128)(2,1)S(1)}, bf16[1,128,2,2,128]{4,1,3,2,0:T(8,128)(2,1)S(1)}, u32[]{:S(2)}, u32[]{:S(2)}) collective-permute-start(bf16[1,128,2,2,128]{4,1,3,2,0:T(8,128)(2,1)S(1)} %get-tuple-element.798), channel_id=1, source_target_pairs={{0,4},{4,8},{8,12},{12,16},{16,20},{20,24},{24,28},{28,32},{32,36}... | collective-permute-start | bytes 393224 | tf_op jit(solution)/shard_map/while/body/eval_jaxpr/ppermute | solution.py:12
  313.4 10.3 %collective-permute-start = (bf16[1,128,2,2,128]{4,1,3,2,0:T(8,128)(2,1)S(1)}, bf16[1,128,2,2,128]{4,1,3,2,0:T(8,128)(2,1)S(1)}, u32[]{:S(2)}, u32[]{:S(2)}) collective-permute-start(bf16[1,128,2,2,128]{4,1,3,2,0:T(8,128)(2,1)S(1)} %get-tuple-element.798), channel_id=1, source_target_pairs={{0,4},{4,8},{8,12},{12,16},{16,20},{20,24},{24,28},{28,32},{32,36}... | collective-permute-start | bytes 393224 | tf_op jit(solution)/shard_map/while/body/eval_jaxpr/ppermute | solution.py:12
  323.7 12.1 %collective-permute-start = (bf16[1,128,2,2,128]{4,1,3,2,0:T(8,128)(2,1)S(1)}, bf16[1,128,2,2,128]{4,1,3,2,0:T(8,128)(2,1)S(1)}, u32[]{:S(2)}, u32[]{:S(2)}) collective-permute-start(bf16[1,128,2,2,128]{4,1,3,2,0:T(8,128)(2,1)S(1)} %get-tuple-element.798), channel_id=1, source_target_pairs={{0,4},{4,8},{8,12},{12,16},{16,20},{20,24},{24,28},{28,32},{32,36}... | collective-permute-start | bytes 393224 | tf_op jit(solution)/shard_map/while/body/eval_jaxpr/ppermute | solution.py:12
  335.9 11.3 %collective-permute-start = (bf16[1,128,2,2,128]{4,1,3,2,0:T(8,128)(2,1)S(1)}, bf16[1,128,2,2,128]{4,1,3,2,0:T(8,128)(2,1)S(1)}, u32[]{:S(2)}, u32[]{:S(2)}) collective-permute-start(bf16[1,128,2,2,128]{4,1,3,2,0:T(8,128)(2,1)S(1)} %get-tuple-element.798), channel_id=1, source_target_pairs={{0,4},{4,8},{8,12},{12,16},{16,20},{20,24},{24,28},{28,32},{32,36}... | collective-permute-start | bytes 393224 | tf_op jit(solution)/shard_map/while/body/eval_jaxpr/ppermute | solution.py:12
  347.3 13.4 %collective-permute-start = (bf16[1,128,2,2,128]{4,1,3,2,0:T(8,128)(2,1)S(1)}, bf16[1,128,2,2,128]{4,1,3,2,0:T(8,128)(2,1)S(1)}, u32[]{:S(2)}, u32[]{:S(2)}) collective-permute-start(bf16[1,128,2,2,128]{4,1,3,2,0:T(8,128)(2,1)S(1)} %get-tuple-element.798), channel_id=1, source_target_pairs={{0,4},{4,8},{8,12},{12,16},{16,20},{20,24},{24,28},{28,32},{32,36}... | collective-permute-start | bytes 393224 | tf_op jit(solution)/shard_map/while/body/eval_jaxpr/ppermute | solution.py:12
  360.7 10.9 %collective-permute-start = (bf16[1,128,2,2,128]{4,1,3,2,0:T(8,128)(2,1)S(1)}, bf16[1,128,2,2,128]{4,1,3,2,0:T(8,128)(2,1)S(1)}, u32[]{:S(2)}, u32[]{:S(2)}) collective-permute-start(bf16[1,128,2,2,128]{4,1,3,2,0:T(8,128)(2,1)S(1)} %get-tuple-element.798), channel_id=1, source_target_pairs={{0,4},{4,8},{8,12},{12,16},{16,20},{20,24},{24,28},{28,32},{32,36}... | collective-permute-start | bytes 393224 | tf_op jit(solution)/shard_map/while/body/eval_jaxpr/ppermute | solution.py:12
  371.6 11.6 %collective-permute-start = (bf16[1,128,2,2,128]{4,1,3,2,0:T(8,128)(2,1)S(1)}, bf16[1,128,2,2,128]{4,1,3,2,0:T(8,128)(2,1)S(1)}, u32[]{:S(2)}, u32[]{:S(2)}) collective-permute-start(bf16[1,128,2,2,128]{4,1,3,2,0:T(8,128)(2,1)S(1)} %get-tuple-element.798), channel_id=1, source_target_pairs={{0,4},{4,8},{8,12},{12,16},{16,20},{20,24},{24,28},{28,32},{32,36}... | collective-permute-start | bytes 393224 | tf_op jit(solution)/shard_map/while/body/eval_jaxpr/ppermute | solution.py:12
  383.3 10.3 %collective-permute-start = (bf16[1,128,2,2,128]{4,1,3,2,0:T(8,128)(2,1)S(1)}, bf16[1,128,2,2,128]{4,1,3,2,0:T(8,128)(2,1)S(1)}, u32[]{:S(2)}, u32[]{:S(2)}) collective-permute-start(bf16[1,128,2,2,128]{4,1,3,2,0:T(8,128)(2,1)S(1)} %get-tuple-element.798), channel_id=1, source_target_pairs={{0,4},{4,8},{8,12},{12,16},{16,20},{20,24},{24,28},{28,32},{32,36}... | collective-permute-start | bytes 393224 | tf_op jit(solution)/shard_map/while/body/eval_jaxpr/ppermute | solution.py:12
  393.7 11.6 %collective-permute-start = (bf16[1,128,2,2,128]{4,1,3,2,0:T(8,128)(2,1)S(1)}, bf16[1,128,2,2,128]{4,1,3,2,0:T(8,128)(2,1)S(1)}, u32[]{:S(2)}, u32[]{:S(2)}) collective-permute-start(bf16[1,128,2,2,128]{4,1,3,2,0:T(8,128)(2,1)S(1)} %get-tuple-element.798), channel_id=1, source_target_pairs={{0,4},{4,8},{8,12},{12,16},{16,20},{20,24},{24,28},{28,32},{32,36}... | collective-permute-start | bytes 393224 | tf_op jit(solution)/shard_map/while/body/eval_jaxpr/ppermute | solution.py:12
  405.3 11.6 %collective-permute-start = (bf16[1,128,2,2,128]{4,1,3,2,0:T(8,128)(2,1)S(1)}, bf16[1,128,2,2,128]{4,1,3,2,0:T(8,128)(2,1)S(1)}, u32[]{:S(2)}, u32[]{:S(2)}) collective-permute-start(bf16[1,128,2,2,128]{4,1,3,2,0:T(8,128)(2,1)S(1)} %get-tuple-element.798), channel_id=1, source_target_pairs={{0,4},{4,8},{8,12},{12,16},{16,20},{20,24},{24,28},{28,32},{32,36}... | collective-permute-start | bytes 393224 | tf_op jit(solution)/shard_map/while/body/eval_jaxpr/ppermute | solution.py:12
  417.0 11.6 %collective-permute-start = (bf16[1,128,2,2,128]{4,1,3,2,0:T(8,128)(2,1)S(1)}, bf16[1,128,2,2,128]{4,1,3,2,0:T(8,128)(2,1)S(1)}, u32[]{:S(2)}, u32[]{:S(2)}) collective-permute-start(bf16[1,128,2,2,128]{4,1,3,2,0:T(8,128)(2,1)S(1)} %get-tuple-element.798), channel_id=1, source_target_pairs={{0,4},{4,8},{8,12},{12,16},{16,20},{20,24},{24,28},{28,32},{32,36}... | collective-permute-start | bytes 393224 | tf_op jit(solution)/shard_map/while/body/eval_jaxpr/ppermute | solution.py:12
  428.6 11.6 %collective-permute-start = (bf16[1,128,2,2,128]{4,1,3,2,0:T(8,128)(2,1)S(1)}, bf16[1,128,2,2,128]{4,1,3,2,0:T(8,128)(2,1)S(1)}, u32[]{:S(2)}, u32[]{:S(2)}) collective-permute-start(bf16[1,128,2,2,128]{4,1,3,2,0:T(8,128)(2,1)S(1)} %get-tuple-element.798), channel_id=1, source_target_pairs={{0,4},{4,8},{8,12},{12,16},{16,20},{20,24},{24,28},{28,32},{32,36}... | collective-permute-start | bytes 393224 | tf_op jit(solution)/shard_map/while/body/eval_jaxpr/ppermute | solution.py:12
  440.3 11.5 %collective-permute-start = (bf16[1,128,2,2,128]{4,1,3,2,0:T(8,128)(2,1)S(1)}, bf16[1,128,2,2,128]{4,1,3,2,0:T(8,128)(2,1)S(1)}, u32[]{:S(2)}, u32[]{:S(2)}) collective-permute-start(bf16[1,128,2,2,128]{4,1,3,2,0:T(8,128)(2,1)S(1)} %get-tuple-element.798), channel_id=1, source_target_pairs={{0,4},{4,8},{8,12},{12,16},{16,20},{20,24},{24,28},{28,32},{32,36}... | collective-permute-start | bytes 393224 | tf_op jit(solution)/shard_map/while/body/eval_jaxpr/ppermute | solution.py:12
  451.8 11.6 %collective-permute-start = (bf16[1,128,2,2,128]{4,1,3,2,0:T(8,128)(2,1)S(1)}, bf16[1,128,2,2,128]{4,1,3,2,0:T(8,128)(2,1)S(1)}, u32[]{:S(2)}, u32[]{:S(2)}) collective-permute-start(bf16[1,128,2,2,128]{4,1,3,2,0:T(8,128)(2,1)S(1)} %get-tuple-element.798), channel_id=1, source_target_pairs={{0,4},{4,8},{8,12},{12,16},{16,20},{20,24},{24,28},{28,32},{32,36}... | collective-permute-start | bytes 393224 | tf_op jit(solution)/shard_map/while/body/eval_jaxpr/ppermute | solution.py:12
  463.5 11.6 %collective-permute-start = (bf16[1,128,2,2,128]{4,1,3,2,0:T(8,128)(2,1)S(1)}, bf16[1,128,2,2,128]{4,1,3,2,0:T(8,128)(2,1)S(1)}, u32[]{:S(2)}, u32[]{:S(2)}) collective-permute-start(bf16[1,128,2,2,128]{4,1,3,2,0:T(8,128)(2,1)S(1)} %get-tuple-element.798), channel_id=1, source_target_pairs={{0,4},{4,8},{8,12},{12,16},{16,20},{20,24},{24,28},{28,32},{32,36}... | collective-permute-start | bytes 393224 | tf_op jit(solution)/shard_map/while/body/eval_jaxpr/ppermute | solution.py:12
  475.1 11.2 %collective-permute-start = (bf16[1,128,2,2,128]{4,1,3,2,0:T(8,128)(2,1)S(1)}, bf16[1,128,2,2,128]{4,1,3,2,0:T(8,128)(2,1)S(1)}, u32[]{:S(2)}, u32[]{:S(2)}) collective-permute-start(bf16[1,128,2,2,128]{4,1,3,2,0:T(8,128)(2,1)S(1)} %get-tuple-element.798), channel_id=1, source_target_pairs={{0,4},{4,8},{8,12},{12,16},{16,20},{20,24},{24,28},{28,32},{32,36}... | collective-permute-start | bytes 393224 | tf_op jit(solution)/shard_map/while/body/eval_jaxpr/ppermute | solution.py:12
  486.4 11.6 %collective-permute-start = (bf16[1,128,2,2,128]{4,1,3,2,0:T(8,128)(2,1)S(1)}, bf16[1,128,2,2,128]{4,1,3,2,0:T(8,128)(2,1)S(1)}, u32[]{:S(2)}, u32[]{:S(2)}) collective-permute-start(bf16[1,128,2,2,128]{4,1,3,2,0:T(8,128)(2,1)S(1)} %get-tuple-element.798), channel_id=1, source_target_pairs={{0,4},{4,8},{8,12},{12,16},{16,20},{20,24},{24,28},{28,32},{32,36}... | collective-permute-start | bytes 393224 | tf_op jit(solution)/shard_map/while/body/eval_jaxpr/ppermute | solution.py:12
  498.0 11.3 %collective-permute-start = (bf16[1,128,2,2,128]{4,1,3,2,0:T(8,128)(2,1)S(1)}, bf16[1,128,2,2,128]{4,1,3,2,0:T(8,128)(2,1)S(1)}, u32[]{:S(2)}, u32[]{:S(2)}) collective-permute-start(bf16[1,128,2,2,128]{4,1,3,2,0:T(8,128)(2,1)S(1)} %get-tuple-element.798), channel_id=1, source_target_pairs={{0,4},{4,8},{8,12},{12,16},{16,20},{20,24},{24,28},{28,32},{32,36}... | collective-permute-start | bytes 393224 | tf_op jit(solution)/shard_map/while/body/eval_jaxpr/ppermute | solution.py:12
  509.4 11.5 %collective-permute-start = (bf16[1,128,2,2,128]{4,1,3,2,0:T(8,128)(2,1)S(1)}, bf16[1,128,2,2,128]{4,1,3,2,0:T(8,128)(2,1)S(1)}, u32[]{:S(2)}, u32[]{:S(2)}) collective-permute-start(bf16[1,128,2,2,128]{4,1,3,2,0:T(8,128)(2,1)S(1)} %get-tuple-element.798), channel_id=1, source_target_pairs={{0,4},{4,8},{8,12},{12,16},{16,20},{20,24},{24,28},{28,32},{32,36}... | collective-permute-start | bytes 393224 | tf_op jit(solution)/shard_map/while/body/eval_jaxpr/ppermute | solution.py:12
  520.9 11.6 %collective-permute-start = (bf16[1,128,2,2,128]{4,1,3,2,0:T(8,128)(2,1)S(1)}, bf16[1,128,2,2,128]{4,1,3,2,0:T(8,128)(2,1)S(1)}, u32[]{:S(2)}, u32[]{:S(2)}) collective-permute-start(bf16[1,128,2,2,128]{4,1,3,2,0:T(8,128)(2,1)S(1)} %get-tuple-element.798), channel_id=1, source_target_pairs={{0,4},{4,8},{8,12},{12,16},{16,20},{20,24},{24,28},{28,32},{32,36}... | collective-permute-start | bytes 393224 | tf_op jit(solution)/shard_map/while/body/eval_jaxpr/ppermute | solution.py:12
  532.6 11.6 %collective-permute-start = (bf16[1,128,2,2,128]{4,1,3,2,0:T(8,128)(2,1)S(1)}, bf16[1,128,2,2,128]{4,1,3,2,0:T(8,128)(2,1)S(1)}, u32[]{:S(2)}, u32[]{:S(2)}) collective-permute-start(bf16[1,128,2,2,128]{4,1,3,2,0:T(8,128)(2,1)S(1)} %get-tuple-element.798), channel_id=1, source_target_pairs={{0,4},{4,8},{8,12},{12,16},{16,20},{20,24},{24,28},{28,32},{32,36}... | collective-permute-start | bytes 393224 | tf_op jit(solution)/shard_map/while/body/eval_jaxpr/ppermute | solution.py:12
  544.2 11.6 %collective-permute-start = (bf16[1,128,2,2,128]{4,1,3,2,0:T(8,128)(2,1)S(1)}, bf16[1,128,2,2,128]{4,1,3,2,0:T(8,128)(2,1)S(1)}, u32[]{:S(2)}, u32[]{:S(2)}) collective-permute-start(bf16[1,128,2,2,128]{4,1,3,2,0:T(8,128)(2,1)S(1)} %get-tuple-element.798), channel_id=1, source_target_pairs={{0,4},{4,8},{8,12},{12,16},{16,20},{20,24},{24,28},{28,32},{32,36}... | collective-permute-start | bytes 393224 | tf_op jit(solution)/shard_map/while/body/eval_jaxpr/ppermute | solution.py:12
  555.8 11.9 %collective-permute-start = (bf16[1,128,2,2,128]{4,1,3,2,0:T(8,128)(2,1)S(1)}, bf16[1,128,2,2,128]{4,1,3,2,0:T(8,128)(2,1)S(1)}, u32[]{:S(2)}, u32[]{:S(2)}) collective-permute-start(bf16[1,128,2,2,128]{4,1,3,2,0:T(8,128)(2,1)S(1)} %get-tuple-element.798), channel_id=1, source_target_pairs={{0,4},{4,8},{8,12},{12,16},{16,20},{20,24},{24,28},{28,32},{32,36}... | collective-permute-start | bytes 393224 | tf_op jit(solution)/shard_map/while/body/eval_jaxpr/ppermute | solution.py:12
  567.7 10.7 %collective-permute-start = (bf16[1,128,2,2,128]{4,1,3,2,0:T(8,128)(2,1)S(1)}, bf16[1,128,2,2,128]{4,1,3,2,0:T(8,128)(2,1)S(1)}, u32[]{:S(2)}, u32[]{:S(2)}) collective-permute-start(bf16[1,128,2,2,128]{4,1,3,2,0:T(8,128)(2,1)S(1)} %get-tuple-element.798), channel_id=1, source_target_pairs={{0,4},{4,8},{8,12},{12,16},{16,20},{20,24},{24,28},{28,32},{32,36}... | collective-permute-start | bytes 393224 | tf_op jit(solution)/shard_map/while/body/eval_jaxpr/ppermute | solution.py:12
  578.4 11.5 %collective-permute-start = (bf16[1,128,2,2,128]{4,1,3,2,0:T(8,128)(2,1)S(1)}, bf16[1,128,2,2,128]{4,1,3,2,0:T(8,128)(2,1)S(1)}, u32[]{:S(2)}, u32[]{:S(2)}) collective-permute-start(bf16[1,128,2,2,128]{4,1,3,2,0:T(8,128)(2,1)S(1)} %get-tuple-element.798), channel_id=1, source_target_pairs={{0,4},{4,8},{8,12},{12,16},{16,20},{20,24},{24,28},{28,32},{32,36}... | collective-permute-start | bytes 393224 | tf_op jit(solution)/shard_map/while/body/eval_jaxpr/ppermute | solution.py:12
  590.0 11.6 %collective-permute-start = (bf16[1,128,2,2,128]{4,1,3,2,0:T(8,128)(2,1)S(1)}, bf16[1,128,2,2,128]{4,1,3,2,0:T(8,128)(2,1)S(1)}, u32[]{:S(2)}, u32[]{:S(2)}) collective-permute-start(bf16[1,128,2,2,128]{4,1,3,2,0:T(8,128)(2,1)S(1)} %get-tuple-element.798), channel_id=1, source_target_pairs={{0,4},{4,8},{8,12},{12,16},{16,20},{20,24},{24,28},{28,32},{32,36}... | collective-permute-start | bytes 393224 | tf_op jit(solution)/shard_map/while/body/eval_jaxpr/ppermute | solution.py:12
  601.7 11.4 %collective-permute-start = (bf16[1,128,2,2,128]{4,1,3,2,0:T(8,128)(2,1)S(1)}, bf16[1,128,2,2,128]{4,1,3,2,0:T(8,128)(2,1)S(1)}, u32[]{:S(2)}, u32[]{:S(2)}) collective-permute-start(bf16[1,128,2,2,128]{4,1,3,2,0:T(8,128)(2,1)S(1)} %get-tuple-element.798), channel_id=1, source_target_pairs={{0,4},{4,8},{8,12},{12,16},{16,20},{20,24},{24,28},{28,32},{32,36}... | collective-permute-start | bytes 393224 | tf_op jit(solution)/shard_map/while/body/eval_jaxpr/ppermute | solution.py:12
  613.0 11.5 %collective-permute-start = (bf16[1,128,2,2,128]{4,1,3,2,0:T(8,128)(2,1)S(1)}, bf16[1,128,2,2,128]{4,1,3,2,0:T(8,128)(2,1)S(1)}, u32[]{:S(2)}, u32[]{:S(2)}) collective-permute-start(bf16[1,128,2,2,128]{4,1,3,2,0:T(8,128)(2,1)S(1)} %get-tuple-element.798), channel_id=1, source_target_pairs={{0,4},{4,8},{8,12},{12,16},{16,20},{20,24},{24,28},{28,32},{32,36}... | collective-permute-start | bytes 393224 | tf_op jit(solution)/shard_map/while/body/eval_jaxpr/ppermute | solution.py:12
  624.6 11.5 %collective-permute-start = (bf16[1,128,2,2,128]{4,1,3,2,0:T(8,128)(2,1)S(1)}, bf16[1,128,2,2,128]{4,1,3,2,0:T(8,128)(2,1)S(1)}, u32[]{:S(2)}, u32[]{:S(2)}) collective-permute-start(bf16[1,128,2,2,128]{4,1,3,2,0:T(8,128)(2,1)S(1)} %get-tuple-element.798), channel_id=1, source_target_pairs={{0,4},{4,8},{8,12},{12,16},{16,20},{20,24},{24,28},{28,32},{32,36}... | collective-permute-start | bytes 393224 | tf_op jit(solution)/shard_map/while/body/eval_jaxpr/ppermute | solution.py:12
  636.1 11.6 %collective-permute-start = (bf16[1,128,2,2,128]{4,1,3,2,0:T(8,128)(2,1)S(1)}, bf16[1,128,2,2,128]{4,1,3,2,0:T(8,128)(2,1)S(1)}, u32[]{:S(2)}, u32[]{:S(2)}) collective-permute-start(bf16[1,128,2,2,128]{4,1,3,2,0:T(8,128)(2,1)S(1)} %get-tuple-element.798), channel_id=1, source_target_pairs={{0,4},{4,8},{8,12},{12,16},{16,20},{20,24},{24,28},{28,32},{32,36}... | collective-permute-start | bytes 393224 | tf_op jit(solution)/shard_map/while/body/eval_jaxpr/ppermute | solution.py:12
  647.7 11.3 %collective-permute-start = (bf16[1,128,2,2,128]{4,1,3,2,0:T(8,128)(2,1)S(1)}, bf16[1,128,2,2,128]{4,1,3,2,0:T(8,128)(2,1)S(1)}, u32[]{:S(2)}, u32[]{:S(2)}) collective-permute-start(bf16[1,128,2,2,128]{4,1,3,2,0:T(8,128)(2,1)S(1)} %get-tuple-element.798), channel_id=1, source_target_pairs={{0,4},{4,8},{8,12},{12,16},{16,20},{20,24},{24,28},{28,32},{32,36}... | collective-permute-start | bytes 393224 | tf_op jit(solution)/shard_map/while/body/eval_jaxpr/ppermute | solution.py:12
  659.1 11.5 %collective-permute-start = (bf16[1,128,2,2,128]{4,1,3,2,0:T(8,128)(2,1)S(1)}, bf16[1,128,2,2,128]{4,1,3,2,0:T(8,128)(2,1)S(1)}, u32[]{:S(2)}, u32[]{:S(2)}) collective-permute-start(bf16[1,128,2,2,128]{4,1,3,2,0:T(8,128)(2,1)S(1)} %get-tuple-element.798), channel_id=1, source_target_pairs={{0,4},{4,8},{8,12},{12,16},{16,20},{20,24},{24,28},{28,32},{32,36}... | collective-permute-start | bytes 393224 | tf_op jit(solution)/shard_map/while/body/eval_jaxpr/ppermute | solution.py:12
  670.6 11.5 %collective-permute-start = (bf16[1,128,2,2,128]{4,1,3,2,0:T(8,128)(2,1)S(1)}, bf16[1,128,2,2,128]{4,1,3,2,0:T(8,128)(2,1)S(1)}, u32[]{:S(2)}, u32[]{:S(2)}) collective-permute-start(bf16[1,128,2,2,128]{4,1,3,2,0:T(8,128)(2,1)S(1)} %get-tuple-element.798), channel_id=1, source_target_pairs={{0,4},{4,8},{8,12},{12,16},{16,20},{20,24},{24,28},{28,32},{32,36}... | collective-permute-start | bytes 393224 | tf_op jit(solution)/shard_map/while/body/eval_jaxpr/ppermute | solution.py:12
  682.1 11.5 %collective-permute-start = (bf16[1,128,2,2,128]{4,1,3,2,0:T(8,128)(2,1)S(1)}, bf16[1,128,2,2,128]{4,1,3,2,0:T(8,128)(2,1)S(1)}, u32[]{:S(2)}, u32[]{:S(2)}) collective-permute-start(bf16[1,128,2,2,128]{4,1,3,2,0:T(8,128)(2,1)S(1)} %get-tuple-element.798), channel_id=1, source_target_pairs={{0,4},{4,8},{8,12},{12,16},{16,20},{20,24},{24,28},{28,32},{32,36}... | collective-permute-start | bytes 393224 | tf_op jit(solution)/shard_map/while/body/eval_jaxpr/ppermute | solution.py:12
  693.6 11.5 %collective-permute-start = (bf16[1,128,2,2,128]{4,1,3,2,0:T(8,128)(2,1)S(1)}, bf16[1,128,2,2,128]{4,1,3,2,0:T(8,128)(2,1)S(1)}, u32[]{:S(2)}, u32[]{:S(2)}) collective-permute-start(bf16[1,128,2,2,128]{4,1,3,2,0:T(8,128)(2,1)S(1)} %get-tuple-element.798), channel_id=1, source_target_pairs={{0,4},{4,8},{8,12},{12,16},{16,20},{20,24},{24,28},{28,32},{32,36}... | collective-permute-start | bytes 393224 | tf_op jit(solution)/shard_map/while/body/eval_jaxpr/ppermute | solution.py:12
  705.1 11.5 %collective-permute-start = (bf16[1,128,2,2,128]{4,1,3,2,0:T(8,128)(2,1)S(1)}, bf16[1,128,2,2,128]{4,1,3,2,0:T(8,128)(2,1)S(1)}, u32[]{:S(2)}, u32[]{:S(2)}) collective-permute-start(bf16[1,128,2,2,128]{4,1,3,2,0:T(8,128)(2,1)S(1)} %get-tuple-element.798), channel_id=1, source_target_pairs={{0,4},{4,8},{8,12},{12,16},{16,20},{20,24},{24,28},{28,32},{32,36}... | collective-permute-start | bytes 393224 | tf_op jit(solution)/shard_map/while/body/eval_jaxpr/ppermute | solution.py:12
  716.6 11.6 %collective-permute-start = (bf16[1,128,2,2,128]{4,1,3,2,0:T(8,128)(2,1)S(1)}, bf16[1,128,2,2,128]{4,1,3,2,0:T(8,128)(2,1)S(1)}, u32[]{:S(2)}, u32[]{:S(2)}) collective-permute-start(bf16[1,128,2,2,128]{4,1,3,2,0:T(8,128)(2,1)S(1)} %get-tuple-element.798), channel_id=1, source_target_pairs={{0,4},{4,8},{8,12},{12,16},{16,20},{20,24},{24,28},{28,32},{32,36}... | collective-permute-start | bytes 393224 | tf_op jit(solution)/shard_map/while/body/eval_jaxpr/ppermute | solution.py:12
  728.3 11.3 %collective-permute-start = (bf16[1,128,2,2,128]{4,1,3,2,0:T(8,128)(2,1)S(1)}, bf16[1,128,2,2,128]{4,1,3,2,0:T(8,128)(2,1)S(1)}, u32[]{:S(2)}, u32[]{:S(2)}) collective-permute-start(bf16[1,128,2,2,128]{4,1,3,2,0:T(8,128)(2,1)S(1)} %get-tuple-element.798), channel_id=1, source_target_pairs={{0,4},{4,8},{8,12},{12,16},{16,20},{20,24},{24,28},{28,32},{32,36}... | collective-permute-start | bytes 393224 | tf_op jit(solution)/shard_map/while/body/eval_jaxpr/ppermute | solution.py:12
  739.6 11.6 %collective-permute-start = (bf16[1,128,2,2,128]{4,1,3,2,0:T(8,128)(2,1)S(1)}, bf16[1,128,2,2,128]{4,1,3,2,0:T(8,128)(2,1)S(1)}, u32[]{:S(2)}, u32[]{:S(2)}) collective-permute-start(bf16[1,128,2,2,128]{4,1,3,2,0:T(8,128)(2,1)S(1)} %get-tuple-element.798), channel_id=1, source_target_pairs={{0,4},{4,8},{8,12},{12,16},{16,20},{20,24},{24,28},{28,32},{32,36}... | collective-permute-start | bytes 393224 | tf_op jit(solution)/shard_map/while/body/eval_jaxpr/ppermute | solution.py:12
  751.3 11.6 %collective-permute-start = (bf16[1,128,2,2,128]{4,1,3,2,0:T(8,128)(2,1)S(1)}, bf16[1,128,2,2,128]{4,1,3,2,0:T(8,128)(2,1)S(1)}, u32[]{:S(2)}, u32[]{:S(2)}) collective-permute-start(bf16[1,128,2,2,128]{4,1,3,2,0:T(8,128)(2,1)S(1)} %get-tuple-element.798), channel_id=1, source_target_pairs={{0,4},{4,8},{8,12},{12,16},{16,20},{20,24},{24,28},{28,32},{32,36}... | collective-permute-start | bytes 393224 | tf_op jit(solution)/shard_map/while/body/eval_jaxpr/ppermute | solution.py:12
  762.9 11.2 %collective-permute-start = (bf16[1,128,2,2,128]{4,1,3,2,0:T(8,128)(2,1)S(1)}, bf16[1,128,2,2,128]{4,1,3,2,0:T(8,128)(2,1)S(1)}, u32[]{:S(2)}, u32[]{:S(2)}) collective-permute-start(bf16[1,128,2,2,128]{4,1,3,2,0:T(8,128)(2,1)S(1)} %get-tuple-element.798), channel_id=1, source_target_pairs={{0,4},{4,8},{8,12},{12,16},{16,20},{20,24},{24,28},{28,32},{32,36}... | collective-permute-start | bytes 393224 | tf_op jit(solution)/shard_map/while/body/eval_jaxpr/ppermute | solution.py:12
  774.1 11.5 %collective-permute-start = (bf16[1,128,2,2,128]{4,1,3,2,0:T(8,128)(2,1)S(1)}, bf16[1,128,2,2,128]{4,1,3,2,0:T(8,128)(2,1)S(1)}, u32[]{:S(2)}, u32[]{:S(2)}) collective-permute-start(bf16[1,128,2,2,128]{4,1,3,2,0:T(8,128)(2,1)S(1)} %get-tuple-element.798), channel_id=1, source_target_pairs={{0,4},{4,8},{8,12},{12,16},{16,20},{20,24},{24,28},{28,32},{32,36}... | collective-permute-start | bytes 393224 | tf_op jit(solution)/shard_map/while/body/eval_jaxpr/ppermute | solution.py:12
  785.6 11.5 %collective-permute-start = (bf16[1,128,2,2,128]{4,1,3,2,0:T(8,128)(2,1)S(1)}, bf16[1,128,2,2,128]{4,1,3,2,0:T(8,128)(2,1)S(1)}, u32[]{:S(2)}, u32[]{:S(2)}) collective-permute-start(bf16[1,128,2,2,128]{4,1,3,2,0:T(8,128)(2,1)S(1)} %get-tuple-element.798), channel_id=1, source_target_pairs={{0,4},{4,8},{8,12},{12,16},{16,20},{20,24},{24,28},{28,32},{32,36}... | collective-permute-start | bytes 393224 | tf_op jit(solution)/shard_map/while/body/eval_jaxpr/ppermute | solution.py:12
  797.1 11.5 %collective-permute-start = (bf16[1,128,2,2,128]{4,1,3,2,0:T(8,128)(2,1)S(1)}, bf16[1,128,2,2,128]{4,1,3,2,0:T(8,128)(2,1)S(1)}, u32[]{:S(2)}, u32[]{:S(2)}) collective-permute-start(bf16[1,128,2,2,128]{4,1,3,2,0:T(8,128)(2,1)S(1)} %get-tuple-element.798), channel_id=1, source_target_pairs={{0,4},{4,8},{8,12},{12,16},{16,20},{20,24},{24,28},{28,32},{32,36}... | collective-permute-start | bytes 393224 | tf_op jit(solution)/shard_map/while/body/eval_jaxpr/ppermute | solution.py:12
  808.6 11.5 %collective-permute-start = (bf16[1,128,2,2,128]{4,1,3,2,0:T(8,128)(2,1)S(1)}, bf16[1,128,2,2,128]{4,1,3,2,0:T(8,128)(2,1)S(1)}, u32[]{:S(2)}, u32[]{:S(2)}) collective-permute-start(bf16[1,128,2,2,128]{4,1,3,2,0:T(8,128)(2,1)S(1)} %get-tuple-element.798), channel_id=1, source_target_pairs={{0,4},{4,8},{8,12},{12,16},{16,20},{20,24},{24,28},{28,32},{32,36}... | collective-permute-start | bytes 393224 | tf_op jit(solution)/shard_map/while/body/eval_jaxpr/ppermute | solution.py:12
  (6 other events, 105.8 us)
Sparse Core Ops, SparseCore 0:
  11.1 29.4 all-gather.2
  44.0 146.7 all-gather.4
  830.9 44.3 reduce-scatter.1
where the time goes:
time: 889 us; the launch traced here: 884 us
  waiting for transfers between devices  749 us (84%)
  other arithmetic  47.9 us (5%)
  loops' own time  44.2 us (5%)
  between operations  15.4 us (2%)
  matrix products  14.7 us (2%)
    ppermute x63, waiting for transfers between devices, from_behind(): lax.ppermute(array, axis, [(i, (i + by) % devices) for i in range(devices)])  683 us
    another operation x1, loops' own time, local(): lax.fori_loop(1, blk_count, cycle_step, (running, cache_pages))  44.1 us
    reduce_scatter x1, waiting for transfers between devices, local(): lax.psum_scatter(jnp.dot(attended, full_out, preferred_element_type=jnp.f...  43.5 us
    reduce_or x64, other arithmetic, visit_one(): jnp.any(matches)  40.7 us
    all_gather x1, waiting for transfers between devices, local(): rows_all = lax.all_gather(normed, 'tp', axis=0, tiled=True)  22 us
  transfers between devices with their start and end apart: 66, of which 65 were waited for; matrix products, arithmetic and copies ran while one was open for 6% of the time, Pallas kernels for 0%

commit v1 on v0

v1 whole, which is shorter than its diff:
```python
import functools

import jax
import jax.numpy as jnp
from jax import lax
from jax.experimental import pallas as pl
from jax.experimental.pallas import tpu as pltpu
from jax.sharding import Mesh, PartitionSpec as P

EPS = 1e-06
THETA = 1000000.0
LOW = -1e30
LOG2E = 1.4426950408889634
MESH = pl.DeviceIdType.MESH
HBM = pl.ANY
BF = jnp.bfloat16


def coords():
    return tuple(lax.axis_index(a) for a in ("y", "zh", "x", "zl", "c"))


def shifted(axis, by):
    me = list(coords())
    me[axis] = lax.rem(me[axis] + by + 4, 4)
    return tuple(me)


def remote(src, dst, sems, n, device):
    return pltpu.make_async_remote_copy(
        src_ref=src, dst_ref=dst, send_sem=sems.at[0, n], recv_sem=sems.at[1, n],
        device_id=device, device_id_type=MESH)


class Ring:
    def __init__(self, me, peer, own, at, half, sems, base):
        self.me, self.peer, self.own, self.at, self.half = me, peer, own, at, half
        self.sems, self.base = sems, base
        self.sent = []

    def slot(self, r):
        return lax.rem(self.me + r + 4, 4)

    def part(self, s, h):
        return self.at(s).at[pl.ds(h * self.half, self.half)]

    def start(self):
        for n, by in ((0, 1), (1, -1)):
            d = remote(self.own, self.at(self.me), self.sems, self.base + n, self.peer(by))
            d.start()
            self.sent.append(d)

    def arrived(self, r):
        n = 0 if r == -1 else 1
        s = self.at(self.slot(r))
        remote(s, s, self.sems, self.base + n, self.peer(1)).wait_recv()

    def forward(self, r):
        h = 0 if r == -1 else 1
        s = self.part(self.slot(r), h)
        d = remote(s, s, self.sems, self.base + 2 + h, self.peer(-r))
        d.start()
        self.sent.append(d)

    def far(self):
        for h in (0, 1):
            s = self.part(self.slot(2), h)
            remote(s, s, self.sems, self.base + 2 + h, self.peer(1)).wait_recv()

    def drain(self):
        for d in self.sent:
            d.wait_send()


def gather_kernel(rows_ref, pages_ref, q_ref, w_ref, rows_all, py, px, qy, qx, w4, sems, lsem):
    y, zh, x, zl, c = coords()
    partner = (y, zh, x, zl, 1 - c)
    across = (y, zh, x, 1 - zl, c)
    barrier = pltpu.get_barrier_semaphore()
    near = [shifted(a, b) for a in (0, 1, 2) for b in (1, -1)] + [partner, across]
    for d in near:
        pl.semaphore_signal(barrier, inc=1, device_id=d, device_id_type=MESH)
    pl.semaphore_wait(barrier, len(near))

    tp = 2 * zl + c
    base = [0]

    def new(me, peer, own, at, half, count=4):
        r = Ring(me, peer, own, at, half, sems, base[0])
        base[0] += count
        return r

    peer_z = lambda by: shifted(1, by)
    peer_y = lambda by: shifted(0, by)
    peer_x = lambda by: shifted(2, by)

    def w_slot(i):
        t = lax.rem(i, 2)
        return w4.at[t, i // 2, x * (1 - t) + y * t]

    def w_ring(r):
        i = lax.rem(zh + r + 4, 4)
        t = lax.rem(i, 2)
        def peer(by):
            return (lax.rem(y + t * by + 4, 4), zh, lax.rem(x + (1 - t) * by + 4, 4), zl, c)
        own = w_ref if r == 0 else w_slot(i)
        return new(x * (1 - t) + y * t, peer, own, lambda s: w4.at[t, i // 2, s], 40)

    def p_ring(r, head):
        i = lax.rem(zh + r + 4, 4)
        buf = px if head else py
        me = y if head else x
        own = pages_ref.at[head] if r == 0 else buf.at[i, me]
        return new(me, peer_y if head else peer_x, own, lambda s: buf.at[i, s], 64)

    zw = new(zh, peer_z, w_ref, w_slot, 40)
    zp = [new(zh, peer_z, pages_ref.at[h], (lambda i: px.at[i, y]) if h else (lambda i: py.at[i, x]), 64)
          for h in (0, 1)]
    local = [
        pltpu.make_async_copy(w_ref, w_slot(zh), lsem.at[0]),
        pltpu.make_async_copy(pages_ref.at[0], py.at[zh, x], lsem.at[1]),
        pltpu.make_async_copy(pages_ref.at[1], px.at[zh, y], lsem.at[2]),
        pltpu.make_async_copy(q_ref.at[0], qy.at[y], lsem.at[3]),
        pltpu.make_async_copy(q_ref.at[1], qx.at[x], lsem.at[4]),
        pltpu.make_async_copy(rows_ref, rows_all.at[tp], lsem.at[5]),
    ]
    b = base[0]
    base[0] += 3
    r_across = remote(rows_ref, rows_all.at[tp], sems, b, across)
    r_partner = remote(rows_ref, rows_all.at[tp], sems, b + 1, partner)
    r_across.start()
    r_partner.start()
    zp[0].start()
    zp[1].start()
    zw.start()
    q_rings = [new(y, peer_y, q_ref.at[0], lambda s: qy.at[s], 64),
               new(x, peer_x, q_ref.at[1], lambda s: qx.at[s], 64)]
    p_own = [p_ring(0, 0), p_ring(0, 1)]
    w_own = w_ring(0)
    rings = [zw] + zp + q_rings + p_own + [w_own]
    for r in p_own + [w_own] + q_rings:
        r.start()
    for d in local:
        d.start()
    there = rows_all.at[2 * (1 - zl) + c]
    remote(there, there, sems, b, across).wait_recv()
    r_pass = remote(there, there, sems, b + 2, partner)
    r_pass.start()

    def step(ring):
        for r in (-1, 1):
            ring.arrived(r)
            ring.forward(r)

    late = []
    for r in (-1, 1):
        for h in (0, 1):
            zp[h].arrived(r)
            zp[h].forward(r)
            ring = p_ring(r, h)
            ring.start()
            late.append(ring)
    for r in p_own:
        step(r)
    for r in (-1, 1):
        zw.arrived(r)
        zw.forward(r)
        ring = w_ring(r)
        ring.start()
        late.append(ring)
    step(w_own)
    for r in q_rings:
        step(r)
    for h in (0, 1):
        zp[h].far()
        ring = p_ring(2, h)
        ring.start()
        late.append(ring)
    for r in late[:4]:
        step(r)
    zw.far()
    ring = w_ring(2)
    ring.start()
    late.append(ring)
    for r in late[4:6]:
        step(r)
    for r in late[6:]:
        step(r)
    for r in q_rings + p_own + [w_own] + late:
        r.far()
    mine = rows_all.at[2 * zl + 1 - c]
    remote(mine, mine, sems, b + 1, partner).wait_recv()
    other = rows_all.at[2 * (1 - zl) + 1 - c]
    remote(other, other, sems, b + 2, partner).wait_recv()
    for r in rings + late:
        r.drain()
    for d in (r_across, r_partner, r_pass):
        d.wait_send()
    for d in local:
        d.wait()
    assert base[0] <= NSEM, base[0]


NSEM = 96


def gather(rows, pages, q, w):
    s = jax.ShapeDtypeStruct
    vm = pl.BlockSpec(memory_space=pltpu.VMEM)
    return pl.pallas_call(
        gather_kernel,
        out_shape=(s((4, 32, 5120), BF), s((4, 4, 128, 256), BF), s((4, 4, 128, 256), BF),
                   s((4, 128, 640), BF), s((4, 128, 640), BF), s((2, 2, 4, 80, 1280), BF)),
        in_specs=[vm] * 4,
        out_specs=[pl.BlockSpec(memory_space=pl.ANY)] * 6,
        scratch_shapes=[pltpu.SemaphoreType.DMA((2, NSEM)), pltpu.SemaphoreType.DMA((6,))],
        compiler_params=pltpu.CompilerParams(collective_id=0, has_side_effects=True),
        name="gather",
    )(rows, pages, q, w)


F32 = jnp.float32
NT = (((1,), (1,)), ((), ()))
TN = (((0,), (0,)), ((), ()))


def attend_kernel(codes, lens, kvp_ref, qy_ref, qx_ref, py_ref, px_ref, trig_ref, reqtrig_ref,
                  o_ref, st_ref, kv_ref, q_s, m_s, l_s, acc_s):
    y, zh, x, zl, c = coords()
    me = y * 16 + zh * 4 + x
    scale = LOG2E * 128 ** -0.5
    lane = lax.broadcasted_iota(jnp.int32, (1, 128), 1)
    sign = jnp.where(lane < 64, -1.0, 1.0).astype(F32)

    def trig(r):
        cl = reqtrig_ref[0, pl.ds(r, 1), :]
        sl = reqtrig_ref[1, pl.ds(r, 1), :]
        ct, st = trig_ref[0], trig_ref[1]
        return cl * ct - sl * st, (sl * ct + cl * st) * sign

    def rope(v, cs):
        return v * cs[0] + pltpu.roll(v, 64, 1) * cs[1]

    cs_own = trig(me)
    for h in range(2):
        kv_ref[:, h * 128:(h + 1) * 128] = rope(kvp_ref[0, :, h * 128:(h + 1) * 128], cs_own).astype(BF)
    kv_ref[:, 256:512] = kvp_ref[1].astype(BF)

    row = lax.broadcasted_iota(jnp.int32, (128, 640), 0)
    col = lax.broadcasted_iota(jnp.int32, (128, 640), 1)

    def update(key, value, keep):
        s = lax.dot_general(key, q_s[...], NT, preferred_element_type=F32) * scale
        s = jnp.where(keep, s, LOW)
        m_old = m_s[0:1, :]
        m_new = jnp.maximum(m_old, jnp.max(s, axis=0, keepdims=True))
        p = jnp.exp2(s - m_new)
        a = jnp.exp2(m_old - m_new)
        l_s[0:1, :] = l_s[0:1, :] * a + jnp.sum(p, axis=0, keepdims=True)
        m_s[0:1, :] = m_new
        acc_s[...] = acc_s[...] * a + lax.dot_general(value, p.astype(BF), TN, preferred_element_type=F32)

    for t in range(2):
        q_ref, p_ref = (qy_ref, py_ref) if t == 0 else (qx_ref, px_ref)
        mine = y if t == 0 else x

        def request_of(i, t=t):
            return i * 16 + zh * 4 + x if t == 0 else y * 16 + zh * 4 + i

        def page_of(s, t=t):
            return y * 16 + s if t == 0 else (s % 4) * 16 + (s // 4) * 4 + x

        def one(i, _, t=t, q_ref=q_ref, p_ref=p_ref, mine=mine, request_of=request_of, page_of=page_of):
            r = request_of(i)

            def count(s, n):
                code = codes[page_of(s)]
                return n + jnp.where((code // 256 == r) & (code % 256 > 0), 1, 0)

            pages = lax.fori_loop(0, 16, count, jnp.int32(0))
            active = (pages > 0) | (i == mine)
            m_s[...] = jnp.full_like(m_s, LOW)
            l_s[...] = jnp.zeros_like(l_s)

            @pl.when(active)
            def _():
                cs = trig(r)
                acc_s[...] = jnp.zeros_like(acc_s)
                for h in range(5):
                    v = q_ref[i, :, h * 128:(h + 1) * 128].astype(F32)
                    q_s[h * 128:(h + 1) * 128, :] = rope(v, cs).astype(BF)

                @pl.when(i == mine)
                def _():
                    update(kv_ref[:, t * 128:(t + 1) * 128], kv_ref[:, 256 + t * 128:384 + t * 128],
                           row <= col % 128)

                def visit(s, z):
                    code = codes[page_of(s)]
                    seen = code % 256

                    @pl.when((code // 256 == r) & (seen > 0))
                    def _():
                        update(p_ref[s, :, 0:128], p_ref[s, :, 128:256], row < seen)

                    return z

                lax.fori_loop(0, 16, visit, 0)
                o_ref[t, i] = (acc_s[...] / l_s[0:1, :]).astype(BF)

            @pl.when(jnp.logical_not(active))
            def _():
                o_ref[t, i] = jnp.zeros((128, 640), BF)

            st_ref[t, i, 0:1, :] = m_s[0:1, :]
            st_ref[t, i, 1:2, :] = l_s[0:1, :]
            return 0

        lax.fori_loop(0, 4, one, 0)


def attend(codes, lens, kvp, qy, qx, py, px, trig, reqtrig):
    s = jax.ShapeDtypeStruct
    vm = pl.BlockSpec(memory_space=pltpu.VMEM)
    sm = pl.BlockSpec(memory_space=pltpu.SMEM)
    return pl.pallas_call(
        attend_kernel,
        out_shape=(s((2, 4, 128, 640), BF), s((2, 4, 8, 640), F32), s((128, 512), BF)),
        in_specs=[sm, sm] + [vm] * 7,
        out_specs=[vm] * 3,
        scratch_shapes=[pltpu.VMEM((640, 128), BF), pltpu.VMEM((8, 640), F32), pltpu.VMEM((8, 640), F32),
                        pltpu.VMEM((128, 640), F32)],
        name="attend",
    )(codes, lens, kvp, qy, qx, py.reshape(16, 128, 256), px.reshape(16, 128, 256), trig, reqtrig)


def project_kernel(o_ref, st_ref, w4_ref, fin, wv, ro, rst, relay, att, ay, ax, part, rc, ps, ra, tot, sems, wsem):
    y, zh, x, zl, c = coords()
    partner = (y, zh, x, zl, 1 - c)
    across = (y, zh, x, 1 - zl, c)
    near = [shifted(a, b) for a in (0, 2) for b in (1, -1, 2)] + [partner, across]
    load = [pltpu.make_async_copy(w4_ref.at[t], wv.at[t], wsem.at[t]) for t in range(2)]
    for d in load:
        d.start()
    barrier = pltpu.get_barrier_semaphore()
    for d in near:
        pl.semaphore_signal(barrier, inc=1, device_id=d, device_id_type=MESH)
    pl.semaphore_wait(barrier, len(near))

    axes = (0, 2)
    mine = (y, x)
    sent = []
    base = [0]

    def send(src, dst, n, device):
        d = remote(src, dst, sems, n, device)
        d.start()
        sent.append(d)

    def got(dst, n):
        remote(dst, dst, sems, n, partner).wait_recv()

    def take(n):
        base[0] += n
        return base[0] - n

    slot = lambda t, r: lax.rem(mine[t] + r + 4, 4)
    d0 = [take(9), take(9)]
    for t in range(2):
        far = o_ref.at[t, slot(t, 2)]
        for h, by in ((0, 1), (1, -1)):
            send(far.at[pl.ds(h * 64, 64)], relay.at[t, h], d0[t] + h, shifted(axes[t], by))
    for t in range(2):
        for h, by in ((0, 1), (1, -1)):
            send(st_ref.at[t, slot(t, by)], rst.at[t, h], d0[t] + 2 + h, shifted(axes[t], by))
        send(st_ref.at[t, slot(t, 2)], rst.at[t, 2], d0[t] + 4, shifted(axes[t], 2))
        for h, by in ((0, 1), (1, -1)):
            send(o_ref.at[t, slot(t, by)], ro.at[t, h], d0[t] + 5 + h, shifted(axes[t], by))
    for t in range(2):
        for h, by in ((0, 1), (1, -1)):
            got(relay.at[t, h], d0[t] + h)
            send(relay.at[t, h], ro.at[t, 2, pl.ds(h * 64, 64)], d0[t] + 7 + h, shifted(axes[t], by))
    for t in range(2):
        for h in (0, 1):
            got(rst.at[t, h], d0[t] + 2 + h)
            got(ro.at[t, h], d0[t] + 5 + h)
            got(ro.at[t, 2, pl.ds(h * 64, 64)], d0[t] + 7 + h)
        got(rst.at[t, 2], d0[t] + 4)
    for t in range(2):
        own = slot(t, 0)
        ms = [st_ref[t, own, 0:1, :]] + [rst[t, i, 0:1, :] for i in range(3)]
        ls = [st_ref[t, own, 1:2, :]] + [rst[t, i, 1:2, :] for i in range(3)]
        top = jnp.maximum(jnp.maximum(ms[0], ms[1]), jnp.maximum(ms[2], ms[3]))
        es = [jnp.exp2(m - top) * l for m, l in zip(ms, ls)]
        inv = 1.0 / (es[0] + es[1] + es[2] + es[3])
        mixed = o_ref[t, own].astype(F32) * (es[0] * inv)
        for i in range(3):
            mixed = mixed + ro[t, i].astype(F32) * (es[i + 1] * inv)
        for h in range(5):
            att[:, (t * 5 + h) * 128:(t * 5 + h + 1) * 128] = mixed[:, h * 128:(h + 1) * 128].T.astype(BF)

    bufs = (ay, ax)
    rings = []
    for t in range(2):
        rings.append(Ring(mine[t], functools.partial(shifted, axes[t]), att, (lambda s, t=t: bufs[t].at[s]), 64,
                          sems, take(4)))
        rings[t].start()
    for d in load:
        d.wait()
    g1, g2, g3 = take(8), take(8), take(8)
    order = (0, -1, 1, 2)

    def multiply(k):
        for t in range(2):
            s = slot(t, order[k])
            a = att[...] if k == 0 else bufs[t][s]
            res = lax.dot_general(a, wv[t].reshape(640, 1280), NT, preferred_element_type=F32).astype(BF)
            for z in range(2):
                for cc in range(2):
                    n = 2 * z + cc
                    part[t, k, cc, z] = res[32 * n:32 * n + 32, :]
            send(part.at[t, k, 1 - c], rc.at[t, k], g1 + 2 * k + t, partner)

    def pair(k):
        for t in range(2):
            got(rc.at[t, k], g1 + 2 * k + t)
            v = part[t, k, c, 1 - zl].astype(F32) + rc[t, k, 1 - zl].astype(F32)
            ps[t, k] = v.astype(BF)
            send(ps.at[t, k], ra.at[t, k], g2 + 2 * k + t, across)

    def finish(k):
        for t in range(2):
            got(ra.at[t, k], g2 + 2 * k + t)
            v = part[t, k, c, zl].astype(F32) + rc[t, k, zl].astype(F32) + ra[t, k].astype(F32)
            if k == 0:
                fin[t, mine[t]] = v.astype(BF)
            else:
                tot[t, k] = v.astype(BF)
                send(tot.at[t, k], fin.at[t, mine[t]], g3 + 2 * k + t, shifted(axes[t], order[k]))

    multiply(0)
    for r in (-1, 1):
        for ring in rings:
            ring.arrived(r)
            ring.forward(r)
    pair(0)
    multiply(1)
    pair(1)
    multiply(2)
    pair(2)
    finish(0)
    finish(1)
    for ring in rings:
        ring.far()
    multiply(3)
    finish(2)
    pair(3)
    finish(3)
    for t in range(2):
        for k in (1, 2, 3):
            got(fin.at[t, slot(t, -order[k])], g3 + 2 * k + t)
    for d in sent:
        d.wait_send()
    for ring in rings:
        ring.drain()
    assert base[0] <= NSEM3, base[0]


NSEM3 = 56


def project(o, st, w4):
    s = jax.ShapeDtypeStruct
    vm = pl.BlockSpec(memory_space=pltpu.VMEM)
    return pl.pallas_call(
        project_kernel,
        out_shape=s((2, 4, 32, 640), BF),
        in_specs=[vm, vm, pl.BlockSpec(memory_space=pl.ANY)],
        out_specs=vm,
        scratch_shapes=[
            pltpu.VMEM((2, 2, 4, 80, 1280), BF), pltpu.VMEM((2, 3, 128, 640), BF), pltpu.VMEM((2, 3, 8, 640), F32),
            pltpu.VMEM((2, 2, 64, 640), BF), pltpu.VMEM((128, 1280), BF), pltpu.VMEM((4, 128, 1280), BF),
            pltpu.VMEM((4, 128, 1280), BF), pltpu.VMEM((2, 4, 2, 2, 32, 640), BF), pltpu.VMEM((2, 4, 2, 32, 640), BF),
            pltpu.VMEM((2, 4, 32, 640), BF), pltpu.VMEM((2, 4, 32, 640), BF), pltpu.VMEM((2, 4, 32, 640), BF),
            pltpu.SemaphoreType.DMA((2, NSEM3)), pltpu.SemaphoreType.DMA((2,))],
        compiler_params=pltpu.CompilerParams(collective_id=1, has_side_effects=True),
        name="project",
    )(o, st, w4)


def page_codes(cached_len, page_table):
    requests, slots = page_table.shape
    r = lax.broadcasted_iota(jnp.int32, (requests, slots), 0)
    j = lax.broadcasted_iota(jnp.int32, (requests, slots), 1)
    seen = jnp.clip(cached_len[:, None] - j * 128, 0, 128)
    value = jnp.where(seen > 0, r * 256 + seen, 0)
    pages = lax.broadcasted_iota(jnp.int32, (64, 1, 1), 0)
    return jnp.sum(jnp.where(page_table[None] == pages, value[None], 0), axis=(1, 2))


def local(hidden_in, norm_gain, kv_weight, kv_bias, queries, cache_pages, out_weight, cached_len, page_table):
    pages = cache_pages[0].transpose(2, 0, 1, 3).reshape(2, 128, 256)
    q = queries.reshape(128, 2, 640).transpose(1, 0, 2)
    rows_all, py, px, qy, qx, w4 = gather(hidden_in, pages, q, out_weight.T)
    codes = page_codes(cached_len, page_table)
    inverse = jnp.power(THETA, -jnp.arange(64, dtype=F32) * 2.0 / 128)
    inverse = jnp.concatenate([inverse, inverse])

    def trig(positions):
        angles = positions.astype(F32)[:, None] * inverse[None, :]
        return jnp.stack([jnp.cos(angles), jnp.sin(angles)])

    hidden_f = rows_all.reshape(128, 5120).astype(F32)
    inverse_rms = lax.rsqrt(jnp.mean(hidden_f * hidden_f, axis=-1, keepdims=True) + EPS)
    normed = (hidden_f * inverse_rms * norm_gain.astype(F32)).astype(BF)
    kvp = jnp.einsum("td,dsc->stc", normed, kv_weight, preferred_element_type=F32)
    kvp = kvp + kv_bias.astype(F32)[:, None, :]
    o, st, kv = attend(codes, cached_len, kvp, qy, qx, py, px, trig(jnp.arange(128)), trig(cached_len))
    fin = project(o, st, w4)
    a = fin[0].reshape(4, 32, 2, 320)
    b = fin[1].reshape(4, 32, 2, 4, 80).transpose(3, 1, 2, 0, 4).reshape(4, 32, 2, 320)
    summed = jnp.stack([a, b], axis=3).transpose(1, 0, 2, 3, 4).reshape(32, 5120)
    hidden_out = (hidden_in.astype(F32) + summed.astype(F32)).astype(BF)
    return hidden_out, kv.reshape(128, 2, 2, 128)


def solution(mesh):
    fine = Mesh(mesh.devices.reshape(4, 4, 4, 2, 2), ("y", "zh", "x", "zl", "c"))
    blk, tp = ("y", "zh", "x"), ("zl", "c")
    in_specs = (P(blk + tp, None), P(), P(None, None, tp), P(None, tp), P(blk, tp),
                P(blk, None, None, tp, None), P(tp, blk), P(), P())
    out_specs = (P(blk + tp, None), P(blk, None, tp, None))
    return jax.shard_map(local, mesh=fine, in_specs=in_specs, out_specs=out_specs, check_vma=False)
```

time: 889 us -> 126 us (0.14)
  waiting for transfers between devices: 749 us -> 0 us
  Pallas kernels: 0 us -> 103 us
  loops' own time: 44.2 us -> 0 us
  other arithmetic: 47.9 us -> 7.96 us
  between operations: 15.4 us -> 0.82 us
  matrix products: 14.7 us -> 4.09 us
    ppermute x63 -> x0, waiting for transfers between devices: 683 us -> none  [from_behind(): lax.ppermute(array, axis, [(i, (i + by) % devices) for i in range(devices)])]
    pallas_call x0 -> x3, Pallas kernels: none -> 103 us  [the longest x1 56 us: gather(): pl.pallas_call(gather_kernel, out_shape=(s((4, 32, 5120), BF), s((4, 4, 1...]
    another operation x65 -> x0, loops' own time: 44.2 us -> none  [the longest x1 44.1 us: local(): lax.fori_loop(1, blk_count, cycle_step, (running, cache_pages))]
    reduce_scatter x1 -> x0, waiting for transfers between devices: 43.5 us -> none  [local(): lax.psum_scatter(jnp.dot(attended, full_out, preferred_element_type=jnp.f...]
    reduce_or x64 -> x0, other arithmetic: 40.7 us -> none  [visit_one(): jnp.any(matches)]
    all_gather x2 -> x0, waiting for transfers between devices: 22 us -> none  [the longest x1 22 us: local(): rows_all = lax.all_gather(normed, 'tp', axis=0, tiled=True)]
    dot_general x4 -> x1, matrix products: 14.7 us -> 4.09 us  [local(): jnp.einsum('td,dsc->stc', normed, kv_weight, preferred_element_type=F32)]
  transfers between devices with their start and end apart: 66 -> 0, of which waited for: 65 -> 0; matrix products, arithmetic and copies ran while one was open for 6% -> 0% of each run, Pallas kernels for 0% -> 0%
where the time goes in v1:
time: 126 us; the launch traced here: 124 us
  Pallas kernels  103 us (82%)
  other arithmetic  7.96 us (6%)
  local copies, waits for them, and re-layouts  7.88 us (6%)
  matrix products  4.09 us (3%)
    pallas_call x1, Pallas kernels, gather(): pl.pallas_call(gather_kernel, out_shape=(s((4, 32, 5120), BF), s((4, 4, 1...  56 us
    pallas_call x1, Pallas kernels, project(): pl.pallas_call(project_kernel, out_shape=s((2, 4, 32, 640), BF), in_specs...  38.9 us
    pallas_call x1, Pallas kernels, attend(): pl.pallas_call(attend_kernel, out_shape=(s((2, 4, 128, 640), BF), s((2, 4...  8.05 us
    dot_general x1, matrix products, local(): jnp.einsum('td,dsc->stc', normed, kv_weight, preferred_element_type=F32)  4.09 us

profile of v1, /device:TPU:1, one launch (start us, length us, event | category | flops | bytes accessed | tf_op | source)
XLA Modules:
  0.0 123.7 jit_solution(16790615321013250805)
XLA Ops:
  0.6 0.0 copy-start.3
  0.6 1.2 copy.31
  1.8 0.9 copy.32
  2.7 1.0 copy.30
  3.7 0.0 copy-start.5
  3.7 0.7 reshape.259.pages_ref
  4.5 56.0 %gather.1 = (bf16[4,32,5120]{2,1,0:T(8,128)(2,1)}, bf16[4,4,128,256]{3,2,1,0:T(8,128)(2,1)}, bf16[4,4,128,256]{3,2,1,0:T(8,128)(2,1)}, bf16[4,128,640]{2,1,0:T(8...) custom-call(bf16[32,5120]{1,0:T(8,128)(2,1)} %rows_ref.1, ...), custom_call_target="tpu_custom_call" | custom-call | tf_op jit(solution)/shard_map/gather/pallas_call | solution.py:210
  60.5 1.7 %multiply_reduce_fusion = f32[4,32]{1,0:T(4,128)S(1)} fusion(bf16[4,32,5120]{2,1,0:T(8,128)(2,1)} %get-tuple-element.11), kind=kLoop, calls=%fused_computation.5 | loop fusion | flops 1965952 | bytes 1311232 | tf_op jit(solution)/shard_map/reduce_sum | solution.py:514
  62.1 0.1 rsqrt.12
  62.2 0.0 copy-done.3
  62.2 1.7 %fusion.3 = bf16[128,5120]{1,0:T(8,128)(2,1)S(1)} fusion(f32[5120]{0:T(1024)S(1)} %convert_element_type.47, f32[128]{0:T(128)S(1)} %rsqrt.12, bf16[4,32,5120]{2,1,0:T(8,128)(2,1)} %get-tuple-element.11), kind=kLoop, calls=%fused_computation.4 | loop fusion | flops 2621440 | bytes 2642432 | tf_op jit(solution)/shard_map/convert_element_type | solution.py:515
  63.9 0.0 copy-done.5
  64.0 0.0 copy-start.4
  64.0 0.0 copy-start.2
  64.0 4.1 %fusion.10.kvp_ref = f32[2,128,256]{2,1,0:T(8,128)} fusion(bf16[5120,2,256]{2,1,0:T(2,128)(2,1)} %param.11, bf16[128,5120]{1,0:T(8,128)(2,1)S(1)} %fusion.3, f32[2,256]{1,0:T(2,128)S(1)} %convert_element_type.49), kind=kOutput, calls=%fused_computation.8 | convolution fusion | flops 671154176 | bytes 6817792 | tf_op jit(solution)/shard_map/td,dsc->stc/dot_general | solution.py:516
  68.1 0.1 pad_maximum_fusion.2
  68.2 0.3 multiply_cosine_fusion
  68.5 0.7 pad_maximum_fusion.trig_ref
  69.2 0.0 copy-done.4
  69.2 0.2 multiply_cosine_fusion.1
  69.4 0.6 pad_maximum_fusion.1.reqtrig_ref
  70.0 0.1 add_select_fusion
  70.1 0.0 copy-done.2
  70.1 1.7 %select_reduce_fusion.codes = s32[64]{0:T(128)} fusion(s32[64,32]{0,1:T(8,128)S(1)} %add_select_fusion, s32[64,32]{0,1:T(8,128)S(1)} %copy-done.2), kind=kLoop, calls=%fused_computation.9 | loop fusion | flops 393152 | bytes 16640 | tf_op jit(solution)/shard_map/reduce_sum | solution.py:498
  71.8 8.1 %attend.1 = (bf16[2,4,128,640]{3,2,1,0:T(8,128)(2,1)}, f32[2,4,8,640]{3,2,1,0:T(8,128)}, bf16[128,512]{1,0:T(8,128)(2,1)}) custom-call(s32[64]{0:T(128)} %select_reduce_fusion.codes, s32[64]{0:T(128)} %lens.1, f32[2,128,256]{2,1,0:T(8,128)} %fusion.10.kvp_ref, bf16[4,128,640]{2,1,0:T(8,128)(2,1)} %get-tuple-element.12.qy_ref, ...), custom_call_target="tpu_custom_call" | custom-call | tf_op jit(solution)/shard_map/attend/pallas_call | solution.py:326
  79.9 38.9 %project.1 = bf16[2,4,32,640]{3,2,1,0:T(8,128)(2,1)} custom-call(bf16[2,4,128,640]{3,2,1,0:T(8,128)(2,1)} %get-tuple-element.16.o_ref, f32[2,4,8,640]{3,2,1,0:T(8,128)} %get-tuple-element.17.st_ref, bf16[2,2,4,80,1280]{4,3,2,1,0:T(8,128)(2,1)} %get-tuple-element.18.w4_ref), custom_call_target="tpu_custom_call" | custom-call | tf_op jit(solution)/shard_map/project/pallas_call | solution.py:475
  118.8 1.0 fusion.16
  119.8 0.3 reshape_squeeze.3
  120.1 0.2 copy.44
  120.3 0.0 copy-start
  120.3 0.2 stack_reshape.3
  120.5 0.2 stack_reshape_squeeze.3
  120.7 0.0 copy-start.1
  120.7 0.1 convert_bitcast_fusion
  120.8 0.6 copy.36
  121.4 0.7 reshape.265
  122.2 0.0 copy-done
  122.2 0.8 add_convert_fusion
  123.0 0.0 copy-done.1
  123.0 0.7 reshape.263
  (9 shorter events, 0.1 us)
Async XLA Ops:
  0.6 61.6 %copy-start.3 = (bf16[5120]{0:T(1024)(128)(2,1)S(1)}, bf16[5120]{0:T(1024)(128)(2,1)}, u32[]{:S(2)}) copy-start(bf16[5120]{0:T(1024)(128)(2,1)} %param.10) | copy-start | bytes 30724
  3.7 60.2 %copy-start.5 = (bf16[2,256]{1,0:T(2,128)(2,1)S(1)}, bf16[2,256]{1,0:T(2,128)(2,1)}, u32[]{:S(2)}) copy-start(bf16[2,256]{1,0:T(2,128)(2,1)} %param.12) | copy-start | bytes 3076
  64.0 5.2 %copy-start.4 = (s32[64]{0:T(128)S(1)}, s32[64]{0:T(128)}, u32[]{:S(2)}) copy-start(s32[64]{0:T(128)} %lens.1) | copy-start | bytes 772
  64.0 6.1 %copy-start.2 = (s32[64,32]{0,1:T(8,128)S(1)}, s32[64,32]{0,1:T(8,128)}, u32[]{:S(2)}) copy-start(s32[64,32]{0,1:T(8,128)} %param.17) | copy-start | bytes 24580
  120.3 1.9 %copy-start = (bf16[32,5120]{1,0:T(8,128)(2,1)S(1)}, bf16[32,5120]{1,0:T(8,128)(2,1)}, u32[]{:S(2)}) copy-start(bf16[32,5120]{1,0:T(8,128)(2,1)} %rows_ref.1) | copy-start | bytes 983044
  120.7 2.3 %copy-start.1 = (bf16[128,512]{1,0:T(8,128)(2,1)S(1)}, bf16[128,512]{1,0:T(8,128)(2,1)}, u32[]{:S(2)}) copy-start(bf16[128,512]{1,0:T(8,128)(2,1)} %get-tuple-element.19) | copy-start | bytes 393220

commit v2 on v1

--- a/solution.py
+++ b/solution.py
@@ -14,6 +14,7 @@
 MESH = pl.DeviceIdType.MESH
 HBM = pl.ANY
 BF = jnp.bfloat16
+F32 = jnp.float32
 
 
 def coords():
@@ -72,7 +73,7 @@
             d.wait_send()
 
 
-def gather_kernel(rows_ref, pages_ref, q_ref, w_ref, rows_all, py, px, qy, qx, w4, sems, lsem):
+def gather_kernel(rows_ref, pages_ref, q_ref, w_ref, gain_ref, normed, py, px, qy, qx, w4, rows_all, sems, lsem):
     y, zh, x, zl, c = coords()
     partner = (y, zh, x, zl, 1 - c)
     across = (y, zh, x, 1 - zl, c)
@@ -111,18 +112,25 @@
         buf = px if head else py
         me = y if head else x
         own = pages_ref.at[head] if r == 0 else buf.at[i, me]
-        return new(me, peer_y if head else peer_x, own, lambda s: buf.at[i, s], 64)
+        return new(me, peer_y if head else peer_x, own, lambda s: buf.at[i, s], 128)
 
     zw = new(zh, peer_z, w_ref, w_slot, 40)
-    zp = [new(zh, peer_z, pages_ref.at[h], (lambda i: px.at[i, y]) if h else (lambda i: py.at[i, x]), 64)
+    zp = [new(zh, peer_z, pages_ref.at[h], (lambda i: px.at[i, y]) if h else (lambda i: py.at[i, x]), 128)
           for h in (0, 1)]
+    def q_part(t):
+        return q_ref.at[:, pl.ds(t * 640, 640)]
+
+    def norm(block, slot):
+        v = block.astype(F32)
+        inverse_rms = lax.rsqrt(jnp.mean(v * v, axis=-1, keepdims=True) + EPS)
+        normed[slot] = (v * inverse_rms * gain_ref[...].astype(F32)).astype(BF)
+
     local = [
         pltpu.make_async_copy(w_ref, w_slot(zh), lsem.at[0]),
         pltpu.make_async_copy(pages_ref.at[0], py.at[zh, x], lsem.at[1]),
         pltpu.make_async_copy(pages_ref.at[1], px.at[zh, y], lsem.at[2]),
-        pltpu.make_async_copy(q_ref.at[0], qy.at[y], lsem.at[3]),
-        pltpu.make_async_copy(q_ref.at[1], qx.at[x], lsem.at[4]),
-        pltpu.make_async_copy(rows_ref, rows_all.at[tp], lsem.at[5]),
+        pltpu.make_async_copy(q_part(0), qy.at[y], lsem.at[3]),
+        pltpu.make_async_copy(q_part(1), qx.at[x], lsem.at[4]),
     ]
     b = base[0]
     base[0] += 3
@@ -133,8 +141,8 @@
     zp[0].start()
     zp[1].start()
     zw.start()
-    q_rings = [new(y, peer_y, q_ref.at[0], lambda s: qy.at[s], 64),
-               new(x, peer_x, q_ref.at[1], lambda s: qx.at[s], 64)]
+    q_rings = [new(y, peer_y, q_part(0), lambda s: qy.at[s], 64),
+               new(x, peer_x, q_part(1), lambda s: qx.at[s], 64)]
     p_own = [p_ring(0, 0), p_ring(0, 1)]
     w_own = w_ring(0)
     rings = [zw] + zp + q_rings + p_own + [w_own]
@@ -142,6 +150,7 @@
         r.start()
     for d in local:
         d.start()
+    norm(rows_ref[...], tp)
     there = rows_all.at[2 * (1 - zl) + c]
     remote(there, there, sems, b, across).wait_recv()
     r_pass = remote(there, there, sems, b + 2, partner)
@@ -186,12 +195,15 @@
         step(r)
     for r in late[6:]:
         step(r)
+    norm(there[...], 2 * (1 - zl) + c)
+    mine = rows_all.at[2 * zl + 1 - c]
+    remote(mine, mine, sems, b + 1, partner).wait_recv()
+    norm(mine[...], 2 * zl + 1 - c)
+    other = rows_all.at[2 * (1 - zl) + 1 - c]
+    remote(other, other, sems, b + 2, partner).wait_recv()
+    norm(other[...], 2 * (1 - zl) + 1 - c)
     for r in q_rings + p_own + [w_own] + late:
         r.far()
-    mine = rows_all.at[2 * zl + 1 - c]
-    remote(mine, mine, sems, b + 1, partner).wait_recv()
-    other = rows_all.at[2 * (1 - zl) + 1 - c]
-    remote(other, other, sems, b + 2, partner).wait_recv()
     for r in rings + late:
         r.drain()
     for d in (r_across, r_partner, r_pass):
@@ -204,27 +216,27 @@
 NSEM = 96
 
 
-def gather(rows, pages, q, w):
+def gather(rows, pages, q, w, gain):
     s = jax.ShapeDtypeStruct
     vm = pl.BlockSpec(memory_space=pltpu.VMEM)
     return pl.pallas_call(
         gather_kernel,
-        out_shape=(s((4, 32, 5120), BF), s((4, 4, 128, 256), BF), s((4, 4, 128, 256), BF),
+        out_shape=(s((4, 32, 5120), BF), s((4, 4, 256, 128), BF), s((4, 4, 256, 128), BF),
                    s((4, 128, 640), BF), s((4, 128, 640), BF), s((2, 2, 4, 80, 1280), BF)),
-        in_specs=[vm] * 4,
-        out_specs=[pl.BlockSpec(memory_space=pl.ANY)] * 6,
-        scratch_shapes=[pltpu.SemaphoreType.DMA((2, NSEM)), pltpu.SemaphoreType.DMA((6,))],
+        in_specs=[vm] * 5,
+        out_specs=[vm] + [pl.BlockSpec(memory_space=pl.ANY)] * 5,
+        scratch_shapes=[pltpu.VMEM((4, 32, 5120), BF), pltpu.SemaphoreType.DMA((2, NSEM)),
+                        pltpu.SemaphoreType.DMA((5,))],
         compiler_params=pltpu.CompilerParams(collective_id=0, has_side_effects=True),
         name="gather",
-    )(rows, pages, q, w)
-
-
-F32 = jnp.float32
+    )(rows, pages, q, w, gain)
+
+
 NT = (((1,), (1,)), ((), ()))
 TN = (((0,), (0,)), ((), ()))
 
 
-def attend_kernel(codes, lens, kvp_ref, qy_ref, qx_ref, py_ref, px_ref, trig_ref, reqtrig_ref,
+def attend_kernel(codes, kvp_ref, qy_ref, qx_ref, py_ref, px_ref, cos_ref, sin_ref,
                   o_ref, st_ref, kv_ref, q_s, m_s, l_s, acc_s):
     y, zh, x, zl, c = coords()
     me = y * 16 + zh * 4 + x
@@ -233,9 +245,9 @@
     sign = jnp.where(lane < 64, -1.0, 1.0).astype(F32)
 
     def trig(r):
-        cl = reqtrig_ref[0, pl.ds(r, 1), :]
-        sl = reqtrig_ref[1, pl.ds(r, 1), :]
-        ct, st = trig_ref[0], trig_ref[1]
+        cl = cos_ref[pl.ds(128 + r, 1), :]
+        sl = sin_ref[pl.ds(128 + r, 1), :]
+        ct, st = cos_ref[0:128, :], sin_ref[0:128, :]
         return cl * ct - sl * st, (sl * ct + cl * st) * sign
 
     def rope(v, cs):
@@ -301,7 +313,7 @@
 
                     @pl.when((code // 256 == r) & (seen > 0))
                     def _():
-                        update(p_ref[s, :, 0:128], p_ref[s, :, 128:256], row < seen)
+                        update(p_ref[s, 0:128, :], p_ref[s, 128:256, :], row < seen)
 
                     return z
 
@@ -319,22 +331,22 @@
         lax.fori_loop(0, 4, one, 0)
 
 
-def attend(codes, lens, kvp, qy, qx, py, px, trig, reqtrig):
+def attend(codes, kvp, qy, qx, py, px, cos, sin):
     s = jax.ShapeDtypeStruct
     vm = pl.BlockSpec(memory_space=pltpu.VMEM)
     sm = pl.BlockSpec(memory_space=pltpu.SMEM)
     return pl.pallas_call(
         attend_kernel,
         out_shape=(s((2, 4, 128, 640), BF), s((2, 4, 8, 640), F32), s((128, 512), BF)),
-        in_specs=[sm, sm] + [vm] * 7,
+        in_specs=[sm] + [vm] * 7,
         out_specs=[vm] * 3,
         scratch_shapes=[pltpu.VMEM((640, 128), BF), pltpu.VMEM((8, 640), F32), pltpu.VMEM((8, 640), F32),
                         pltpu.VMEM((128, 640), F32)],
         name="attend",
-    )(codes, lens, kvp, qy, qx, py.reshape(16, 128, 256), px.reshape(16, 128, 256), trig, reqtrig)
-
-
-def project_kernel(o_ref, st_ref, w4_ref, fin, wv, ro, rst, relay, att, ay, ax, part, rc, ps, ra, tot, sems, wsem):
+    )(codes, kvp, qy, qx, py.reshape(16, 256, 128), px.reshape(16, 256, 128), cos, sin)
+
+
+def project_kernel(o_ref, st_ref, w4_ref, hid_ref, out_ref, fin, wv, ro, rst, relay, att, ay, ax, part, rc, ps, ra, tot, sems, wsem):
     y, zh, x, zl, c = coords()
     partner = (y, zh, x, zl, 1 - c)
     across = (y, zh, x, 1 - zl, c)
@@ -459,6 +471,15 @@
     for t in range(2):
         for k in (1, 2, 3):
             got(fin.at[t, slot(t, -order[k])], g3 + 2 * k + t)
+    for u in range(4):
+        for g in range(2):
+            pieces = [fin[0, u].astype(F32)[:, g * 320:g * 320 + 320]]
+            for s in range(4):
+                first = g * 320 + u * 80
+                pieces.append(fin[1, s].astype(F32)[:, first:first + 80])
+            cols = pl.ds(u * 1280 + g * 640, 640)
+            summed = jnp.concatenate(pieces, axis=1)
+            out_ref[:, cols] = (hid_ref[:, cols].astype(F32) + summed).astype(BF)
     for d in sent:
         d.wait_send()
     for ring in rings:
@@ -469,15 +490,16 @@
 NSEM3 = 56
 
 
-def project(o, st, w4):
+def project(o, st, w4, hidden):
     s = jax.ShapeDtypeStruct
     vm = pl.BlockSpec(memory_space=pltpu.VMEM)
     return pl.pallas_call(
         project_kernel,
-        out_shape=s((2, 4, 32, 640), BF),
-        in_specs=[vm, vm, pl.BlockSpec(memory_space=pl.ANY)],
+        out_shape=s((32, 5120), BF),
+        in_specs=[vm, vm, pl.BlockSpec(memory_space=pl.ANY), vm],
         out_specs=vm,
         scratch_shapes=[
+            pltpu.VMEM((2, 4, 32, 640), BF),
             pltpu.VMEM((2, 2, 4, 80, 1280), BF), pltpu.VMEM((2, 3, 128, 640), BF), pltpu.VMEM((2, 3, 8, 640), F32),
             pltpu.VMEM((2, 2, 64, 640), BF), pltpu.VMEM((128, 1280), BF), pltpu.VMEM((4, 128, 1280), BF),
             pltpu.VMEM((4, 128, 1280), BF), pltpu.VMEM((2, 4, 2, 2, 32, 640), BF), pltpu.VMEM((2, 4, 2, 32, 640), BF),
@@ -485,7 +507,7 @@
             pltpu.SemaphoreType.DMA((2, NSEM3)), pltpu.SemaphoreType.DMA((2,))],
         compiler_params=pltpu.CompilerParams(collective_id=1, has_side_effects=True),
         name="project",
-    )(o, st, w4)
+    )(o, st, w4, hidden)
 
 
 def page_codes(cached_len, page_table):
@@ -493,35 +515,23 @@
     r = lax.broadcasted_iota(jnp.int32, (requests, slots), 0)
     j = lax.broadcasted_iota(jnp.int32, (requests, slots), 1)
     seen = jnp.clip(cached_len[:, None] - j * 128, 0, 128)
-    value = jnp.where(seen > 0, r * 256 + seen, 0)
-    pages = lax.broadcasted_iota(jnp.int32, (64, 1, 1), 0)
-    return jnp.sum(jnp.where(page_table[None] == pages, value[None], 0), axis=(1, 2))
+    value = jnp.where(seen > 0, r * 256 + seen, 0).reshape(1, -1)
+    pages = lax.broadcasted_iota(jnp.int32, (64, 1), 0)
+    return jnp.sum(jnp.where(page_table.reshape(1, -1) == pages, value, 0), axis=1)
 
 
 def local(hidden_in, norm_gain, kv_weight, kv_bias, queries, cache_pages, out_weight, cached_len, page_table):
-    pages = cache_pages[0].transpose(2, 0, 1, 3).reshape(2, 128, 256)
-    q = queries.reshape(128, 2, 640).transpose(1, 0, 2)
-    rows_all, py, px, qy, qx, w4 = gather(hidden_in, pages, q, out_weight.T)
+    pages = cache_pages[0].transpose(2, 1, 0, 3).reshape(2, 256, 128)
+    normed, py, px, qy, qx, w4 = gather(hidden_in, pages, queries, out_weight.T, norm_gain.reshape(1, 5120))
     codes = page_codes(cached_len, page_table)
-    inverse = jnp.power(THETA, -jnp.arange(64, dtype=F32) * 2.0 / 128)
-    inverse = jnp.concatenate([inverse, inverse])
-
-    def trig(positions):
-        angles = positions.astype(F32)[:, None] * inverse[None, :]
-        return jnp.stack([jnp.cos(angles), jnp.sin(angles)])
-
-    hidden_f = rows_all.reshape(128, 5120).astype(F32)
-    inverse_rms = lax.rsqrt(jnp.mean(hidden_f * hidden_f, axis=-1, keepdims=True) + EPS)
-    normed = (hidden_f * inverse_rms * norm_gain.astype(F32)).astype(BF)
-    kvp = jnp.einsum("td,dsc->stc", normed, kv_weight, preferred_element_type=F32)
+    pair = lax.broadcasted_iota(jnp.int32, (1, 128), 1) % 64
+    inverse = jnp.power(THETA, -pair.astype(F32) * 2.0 / 128)
+    positions = jnp.concatenate([jnp.arange(128, dtype=jnp.int32), cached_len])
+    angles = positions.astype(F32)[:, None] * inverse
+    kvp = jnp.einsum("td,dsc->stc", normed.reshape(128, 5120), kv_weight, preferred_element_type=F32)
     kvp = kvp + kv_bias.astype(F32)[:, None, :]
-    o, st, kv = attend(codes, cached_len, kvp, qy, qx, py, px, trig(jnp.arange(128)), trig(cached_len))
-    fin = project(o, st, w4)
-    a = fin[0].reshape(4, 32, 2, 320)
-    b = fin[1].reshape(4, 32, 2, 4, 80).transpose(3, 1, 2, 0, 4).reshape(4, 32, 2, 320)
-    summed = jnp.stack([a, b], axis=3).transpose(1, 0, 2, 3, 4).reshape(32, 5120)
-    hidden_out = (hidden_in.astype(F32) + summed.astype(F32)).astype(BF)
-    return hidden_out, kv.reshape(128, 2, 2, 128)
+    o, st, kv = attend(codes, kvp, qy, qx, py, px, jnp.cos(angles), jnp.sin(angles))
+    return project(o, st, w4, hidden_in), kv.reshape(128, 2, 2, 128)
 
 
 def solution(mesh):

time: 126 us -> 124 us (0.984)
  the two profiles are of different devices: /device:TPU:1 before, /device:TPU:192 now
where the time goes in v2:
time: 124 us; the launch traced here: 123 us
  Pallas kernels  108 us (87%)
  local copies, waits for them, and re-layouts  6.25 us (5%)
  matrix products  4.46 us (4%)
  other arithmetic  3.86 us (3%)
    pallas_call x1, Pallas kernels, gather(): pl.pallas_call(gather_kernel, out_shape=(s((4, 32, 5120), BF), s((4, 4, 2...  53.6 us
    pallas_call x1, Pallas kernels, project(): pl.pallas_call(project_kernel, out_shape=s((32, 5120), BF), in_specs=[vm,...  45.8 us
    pallas_call x1, Pallas kernels, attend(): pl.pallas_call(attend_kernel, out_shape=(s((2, 4, 128, 640), BF), s((2, 4...  8.78 us
    dot_general x1, matrix products, local(): jnp.einsum('td,dsc->stc', normed.reshape(128, 5120), kv_weight, preferred...  4.46 us
    unnamed x4, local copies, waits for them, and re-layouts  2.52 us

profile of v2, /device:TPU:192, one launch (start us, length us, event | category | flops | bytes accessed | tf_op | source)
XLA Modules:
  0.0 123.5 jit_solution(8254503777878020917)
XLA Ops:
  0.7 0.7 add_convert_fusion
  1.3 0.7 convert_element_type.18
  2.0 1.3 %reshape.96.gain_ref = bf16[1,5120]{1,0:T(2,128)(2,1)} reshape(bf16[5120]{0:T(1024)(128)(2,1)} %param.10) | data formatting | bytes 20480 | tf_op jit(solution)/shard_map/reshape | solution.py:525
  3.3 0.7 add_select_fusion
  4.1 0.1 select_n.28
  4.2 0.8 copy.16
  5.0 0.1 eq.17
  5.0 0.6 select_reduce_fusion.codes
  5.7 1.6 %copy.17 = bf16[2,2,128,128]{3,2,1,0:T(8,128)(2,1)} copy(bf16[2,2,128,128]{3,0,1,2:T(2,128)(2,1)} %bitcast.17) | data formatting | bytes 262144 | tf_op jit(solution)/shard_map/transpose | solution.py:524
  7.3 1.1 multiply_sine_fusion
  8.4 53.6 %gather.1 = (bf16[4,32,5120]{2,1,0:T(8,128)(2,1)}, bf16[4,4,256,128]{3,2,1,0:T(8,128)(2,1)}, bf16[4,4,256,128]{3,2,1,0:T(8,128)(2,1)}, bf16[4,128,640]{2,1,0:T(8...) custom-call(bf16[32,5120]{1,0:T(8,128)(2,1)} %hid_ref.1, bf16[2,256,128]{2,1,0:T(8,128)(2,1)} %bitcast.15, ...), custom_call_target="tpu_custom_call" | custom-call | tf_op jit(solution)/shard_map/gather/pallas_call | solution.py:222
  62.0 4.5 %fusion.5.kvp_ref = f32[2,128,256]{2,1,0:T(8,128)} fusion(bf16[128,5120,1]{1,0,2:T(8,128)(2,1)} %bitcast.18, bf16[5120,2,256]{2,1,0:T(2,128)(2,1)} %param.11, f32[2,256]{1,0:T(2,128)S(1)} %convert_element_type.18), kind=kOutput, calls=%fused_computation.3 | convolution fusion | flops 671154176 | bytes 6817792 | tf_op jit(solution)/shard_map/td,dsc->stc/dot_general | solution.py:531
  66.4 8.8 %attend.1 = (bf16[2,4,128,640]{3,2,1,0:T(8,128)(2,1)}, f32[2,4,8,640]{3,2,1,0:T(8,128)}, bf16[128,512]{1,0:T(8,128)(2,1)}) custom-call(s32[64]{0:T(128)} %select_reduce_fusion.codes, f32[2,128,256]{2,1,0:T(8,128)} %fusion.5.kvp_ref, bf16[4,128,640]{2,1,0:T(8,128)(2,1)} %get-tuple-element.12.qy_ref, bf16[4,128,640]{2,1,0:T(8,128)(2,1)} %get-tuple-element.13.qx_ref, ...), custom_call_target="tpu_custom_call" | custom-call | tf_op jit(solution)/shard_map/attend/pallas_call | solution.py:338
  75.2 0.0 copy-start
  75.2 45.8 %project.1 = bf16[32,5120]{1,0:T(8,128)(2,1)} custom-call(bf16[2,4,128,640]{3,2,1,0:T(8,128)(2,1)} %get-tuple-element.16.o_ref, f32[2,4,8,640]{3,2,1,0:T(8,128)} %get-tuple-element.17.st_ref, bf16[2,2,4,80,1280]{4,3,2,1,0:T(8,128)(2,1)} %get-tuple-element.18.w4_ref, bf16[32,5120]{1,0:T(8,128)(2,1)} %hid_ref.1), custom_call_target="tpu_custom_call" | custom-call | tf_op jit(solution)/shard_map/project/pallas_call | solution.py:496
  121.0 0.0 copy-done
  121.0 0.7 reshape.100
  121.7 1.7 %copy.26 = bf16[32,5120]{1,0:T(8,128)(2,1)} copy(bf16[32,5120]{1,0:T(8,128)(2,1)} %project.1) | data formatting | bytes 655360
  (4 shorter events, 0.0 us)
Async XLA Ops:
  75.2 45.8 %copy-start = (bf16[128,512]{1,0:T(8,128)(2,1)S(1)}, bf16[128,512]{1,0:T(8,128)(2,1)}, u32[]{:S(2)}) copy-start(bf16[128,512]{1,0:T(8,128)(2,1)} %get-tuple-element.19) | copy-start | bytes 393220

commit v3 on v2

--- a/solution.py
+++ b/solution.py
@@ -73,7 +73,8 @@
             d.wait_send()
 
 
-def gather_kernel(rows_ref, pages_ref, q_ref, w_ref, gain_ref, normed, py, px, qy, qx, w4, rows_all, sems, lsem):
+def gather_kernel(rows_ref, pages_ref, q_ref, w_ref, gain_ref, table_ref, value_ref, normed, py, px, qy, qx, w4,
+                  codes, rows_all, sems, lsem):
     y, zh, x, zl, c = coords()
     partner = (y, zh, x, zl, 1 - c)
     across = (y, zh, x, 1 - zl, c)
@@ -123,7 +124,19 @@
     def norm(block, slot):
         v = block.astype(F32)
         inverse_rms = lax.rsqrt(jnp.mean(v * v, axis=-1, keepdims=True) + EPS)
-        normed[slot] = (v * inverse_rms * gain_ref[...].astype(F32)).astype(BF)
+        v = v * inverse_rms
+        for k in range(40):
+            cols = pl.ds(k * 128, 128)
+            normed[slot, :, cols] = (v[:, k * 128:k * 128 + 128] * gain_ref[k:k + 1, :].astype(F32)).astype(BF)
+
+    def find_codes():
+        table, value = table_ref[...], value_ref[...]
+        row = lax.broadcasted_iota(jnp.int32, (64, 128), 0)
+        lane = lax.broadcasted_iota(jnp.int32, (64, 128), 1)
+        rows = [jnp.sum(jnp.where(table == p, value, 0), axis=0, keepdims=True) for p in range(64)]
+        each = jnp.sum(jnp.concatenate(rows, axis=0), axis=1, keepdims=True)
+        codes[0:1, :] = jnp.sum(jnp.where(row == lane, each, 0), axis=0, keepdims=True)
+        codes[1:8, :] = jnp.zeros((7, 128), jnp.int32)
 
     local = [
         pltpu.make_async_copy(w_ref, w_slot(zh), lsem.at[0]),
@@ -136,11 +149,10 @@
     base[0] += 3
     r_across = remote(rows_ref, rows_all.at[tp], sems, b, across)
     r_partner = remote(rows_ref, rows_all.at[tp], sems, b + 1, partner)
-    r_across.start()
-    r_partner.start()
     zp[0].start()
     zp[1].start()
     zw.start()
+    r_partner.start()
     q_rings = [new(y, peer_y, q_part(0), lambda s: qy.at[s], 64),
                new(x, peer_x, q_part(1), lambda s: qx.at[s], 64)]
     p_own = [p_ring(0, 0), p_ring(0, 1)]
@@ -152,9 +164,8 @@
         d.start()
     norm(rows_ref[...], tp)
     there = rows_all.at[2 * (1 - zl) + c]
-    remote(there, there, sems, b, across).wait_recv()
-    r_pass = remote(there, there, sems, b + 2, partner)
-    r_pass.start()
+    mine = rows_all.at[2 * zl + 1 - c]
+    other = rows_all.at[2 * (1 - zl) + 1 - c]
 
     def step(ring):
         for r in (-1, 1):
@@ -162,44 +173,49 @@
             ring.forward(r)
 
     late = []
+
+    def begin(ring):
+        ring.start()
+        late.append(ring)
+        return ring
+
+    for r in p_own:
+        step(r)
+    p_near = []
     for r in (-1, 1):
         for h in (0, 1):
             zp[h].arrived(r)
             zp[h].forward(r)
-            ring = p_ring(r, h)
-            ring.start()
-            late.append(ring)
-    for r in p_own:
+            p_near.append(begin(p_ring(r, h)))
+    step(w_own)
+    for r in q_rings:
         step(r)
+    for r in p_near:
+        step(r)
+    w_near = []
     for r in (-1, 1):
         zw.arrived(r)
         zw.forward(r)
-        ring = w_ring(r)
-        ring.start()
-        late.append(ring)
-    step(w_own)
-    for r in q_rings:
-        step(r)
+        w_near.append(begin(w_ring(r)))
+    r_across.start()
+    remote(mine, mine, sems, b + 1, partner).wait_recv()
+    norm(mine[...], 2 * zl + 1 - c)
+    find_codes()
+    p_far = []
     for h in (0, 1):
         zp[h].far()
-        ring = p_ring(2, h)
-        ring.start()
-        late.append(ring)
-    for r in late[:4]:
+        p_far.append(begin(p_ring(2, h)))
+    step(w_near[0])
+    zw.far()
+    w_far = begin(w_ring(2))
+    step(w_near[1])
+    for r in p_far:
         step(r)
-    zw.far()
-    ring = w_ring(2)
-    ring.start()
-    late.append(ring)
-    for r in late[4:6]:
-        step(r)
-    for r in late[6:]:
-        step(r)
+    remote(there, there, sems, b, across).wait_recv()
+    r_pass = remote(there, there, sems, b + 2, partner)
+    r_pass.start()
     norm(there[...], 2 * (1 - zl) + c)
-    mine = rows_all.at[2 * zl + 1 - c]
-    remote(mine, mine, sems, b + 1, partner).wait_recv()
-    norm(mine[...], 2 * zl + 1 - c)
-    other = rows_all.at[2 * (1 - zl) + 1 - c]
+    step(w_far)
     remote(other, other, sems, b + 2, partner).wait_recv()
     norm(other[...], 2 * (1 - zl) + 1 - c)
     for r in q_rings + p_own + [w_own] + late:
@@ -216,27 +232,28 @@
 NSEM = 96
 
 
-def gather(rows, pages, q, w, gain):
+def gather(rows, pages, q, w, gain, table, value):
     s = jax.ShapeDtypeStruct
     vm = pl.BlockSpec(memory_space=pltpu.VMEM)
     return pl.pallas_call(
         gather_kernel,
         out_shape=(s((4, 32, 5120), BF), s((4, 4, 256, 128), BF), s((4, 4, 256, 128), BF),
-                   s((4, 128, 640), BF), s((4, 128, 640), BF), s((2, 2, 4, 80, 1280), BF)),
-        in_specs=[vm] * 5,
-        out_specs=[vm] + [pl.BlockSpec(memory_space=pl.ANY)] * 5,
+                   s((4, 128, 640), BF), s((4, 128, 640), BF), s((2, 2, 4, 80, 1280), BF),
+                   s((8, 128), jnp.int32)),
+        in_specs=[vm] * 7,
+        out_specs=[vm] + [pl.BlockSpec(memory_space=pl.ANY)] * 5 + [vm],
         scratch_shapes=[pltpu.VMEM((4, 32, 5120), BF), pltpu.SemaphoreType.DMA((2, NSEM)),
                         pltpu.SemaphoreType.DMA((5,))],
         compiler_params=pltpu.CompilerParams(collective_id=0, has_side_effects=True),
         name="gather",
-    )(rows, pages, q, w, gain)
+    )(rows, pages, q, w, gain, table, value)
 
 
 NT = (((1,), (1,)), ((), ()))
 TN = (((0,), (0,)), ((), ()))
 
 
-def attend_kernel(codes, kvp_ref, qy_ref, qx_ref, py_ref, px_ref, cos_ref, sin_ref,
+def attend_kernel(codes, kvp_ref, qy_ref, qx_ref, py_ref, px_ref, cos_ref, sin_ref, rcos_ref, rsin_ref,
                   o_ref, st_ref, kv_ref, q_s, m_s, l_s, acc_s):
     y, zh, x, zl, c = coords()
     me = y * 16 + zh * 4 + x
@@ -245,9 +262,9 @@
     sign = jnp.where(lane < 64, -1.0, 1.0).astype(F32)
 
     def trig(r):
-        cl = cos_ref[pl.ds(128 + r, 1), :]
-        sl = sin_ref[pl.ds(128 + r, 1), :]
-        ct, st = cos_ref[0:128, :], sin_ref[0:128, :]
+        cl = rcos_ref[pl.ds(r, 1), :]
+        sl = rsin_ref[pl.ds(r, 1), :]
+        ct, st = cos_ref[...], sin_ref[...]
         return cl * ct - sl * st, (sl * ct + cl * st) * sign
 
     def rope(v, cs):
@@ -286,7 +303,7 @@
             r = request_of(i)
 
             def count(s, n):
-                code = codes[page_of(s)]
+                code = codes[0, page_of(s)]
                 return n + jnp.where((code // 256 == r) & (code % 256 > 0), 1, 0)
 
             pages = lax.fori_loop(0, 16, count, jnp.int32(0))
@@ -308,7 +325,7 @@
                            row <= col % 128)
 
                 def visit(s, z):
-                    code = codes[page_of(s)]
+                    code = codes[0, page_of(s)]
                     seen = code % 256
 
                     @pl.when((code // 256 == r) & (seen > 0))
@@ -331,19 +348,19 @@
         lax.fori_loop(0, 4, one, 0)
 
 
-def attend(codes, kvp, qy, qx, py, px, cos, sin):
+def attend(codes, kvp, qy, qx, py, px, trigs):
     s = jax.ShapeDtypeStruct
     vm = pl.BlockSpec(memory_space=pltpu.VMEM)
     sm = pl.BlockSpec(memory_space=pltpu.SMEM)
     return pl.pallas_call(
         attend_kernel,
         out_shape=(s((2, 4, 128, 640), BF), s((2, 4, 8, 640), F32), s((128, 512), BF)),
-        in_specs=[sm] + [vm] * 7,
+        in_specs=[sm] + [vm] * 9,
         out_specs=[vm] * 3,
         scratch_shapes=[pltpu.VMEM((640, 128), BF), pltpu.VMEM((8, 640), F32), pltpu.VMEM((8, 640), F32),
                         pltpu.VMEM((128, 640), F32)],
         name="attend",
-    )(codes, kvp, qy, qx, py.reshape(16, 256, 128), px.reshape(16, 256, 128), cos, sin)
+    )(codes, kvp, qy, qx, py.reshape(16, 256, 128), px.reshape(16, 256, 128), *trigs)
 
 
 def project_kernel(o_ref, st_ref, w4_ref, hid_ref, out_ref, fin, wv, ro, rst, relay, att, ay, ax, part, rc, ps, ra, tot, sems, wsem):
@@ -510,27 +527,27 @@
     )(o, st, w4, hidden)
 
 
-def page_codes(cached_len, page_table):
-    requests, slots = page_table.shape
-    r = lax.broadcasted_iota(jnp.int32, (requests, slots), 0)
-    j = lax.broadcasted_iota(jnp.int32, (requests, slots), 1)
+def entry_values(cached_len, shape):
+    r = lax.broadcasted_iota(jnp.int32, shape, 0)
+    j = lax.broadcasted_iota(jnp.int32, shape, 1)
     seen = jnp.clip(cached_len[:, None] - j * 128, 0, 128)
-    value = jnp.where(seen > 0, r * 256 + seen, 0).reshape(1, -1)
-    pages = lax.broadcasted_iota(jnp.int32, (64, 1), 0)
-    return jnp.sum(jnp.where(page_table.reshape(1, -1) == pages, value, 0), axis=1)
+    return jnp.where(seen > 0, r * 256 + seen, 0)
 
 
 def local(hidden_in, norm_gain, kv_weight, kv_bias, queries, cache_pages, out_weight, cached_len, page_table):
     pages = cache_pages[0].transpose(2, 1, 0, 3).reshape(2, 256, 128)
-    normed, py, px, qy, qx, w4 = gather(hidden_in, pages, queries, out_weight.T, norm_gain.reshape(1, 5120))
-    codes = page_codes(cached_len, page_table)
+    normed, py, px, qy, qx, w4, codes = gather(
+        hidden_in, pages, queries, out_weight.T, norm_gain.reshape(40, 128),
+        page_table, entry_values(cached_len, page_table.shape))
     pair = lax.broadcasted_iota(jnp.int32, (1, 128), 1) % 64
     inverse = jnp.power(THETA, -pair.astype(F32) * 2.0 / 128)
-    positions = jnp.concatenate([jnp.arange(128, dtype=jnp.int32), cached_len])
-    angles = positions.astype(F32)[:, None] * inverse
+    trigs = []
+    for positions in (jnp.arange(128), cached_len):
+        angles = positions.astype(F32)[:, None] * inverse
+        trigs += [jnp.cos(angles), jnp.sin(angles)]
     kvp = jnp.einsum("td,dsc->stc", normed.reshape(128, 5120), kv_weight, preferred_element_type=F32)
     kvp = kvp + kv_bias.astype(F32)[:, None, :]
-    o, st, kv = attend(codes, kvp, qy, qx, py, px, jnp.cos(angles), jnp.sin(angles))
+    o, st, kv = attend(codes, kvp, qy, qx, py, px, trigs)
     return project(o, st, w4, hidden_in), kv.reshape(128, 2, 2, 128)
 
 

time: 124 us -> 118 us (0.952)
  the two profiles are of different devices: /device:TPU:192 before, /device:TPU:64 now
where the time goes in v3:
time: 118 us
  Pallas kernels  103 us (87%)
  local copies, waits for them, and re-layouts  5.4 us (5%)
  other arithmetic  4.51 us (4%)
  matrix products  4.46 us (4%)
    pallas_call x1, Pallas kernels, gather(): pl.pallas_call(gather_kernel, out_shape=(s((4, 32, 5120), BF), s((4, 4, 2...  46.7 us
    pallas_call x1, Pallas kernels, project(): pl.pallas_call(project_kernel, out_shape=s((32, 5120), BF), in_specs=[vm,...  42.5 us
    pallas_call x1, Pallas kernels, attend(): pl.pallas_call(attend_kernel, out_shape=(s((2, 4, 128, 640), BF), s((2, 4...  13.4 us
    dot_general x1, matrix products, local(): jnp.einsum('td,dsc->stc', normed.reshape(128, 5120), kv_weight, preferred...  4.46 us
    unnamed x4, local copies, waits for them, and re-layouts  3.13 us

profile of v3, /device:TPU:64, one launch (start us, length us, event | category | flops | bytes accessed | tf_op | source)
XLA Modules:
  0.0 117.6 jit_solution(13732021510681970947)
XLA Ops:
  0.6 0.7 convert_element_type.30
  1.3 0.7 convert_element_type.27
  2.0 1.3 %add_select_fusion.value_ref = s32[64,32]{1,0:T(8,128)} fusion(s32[64]{0:T(128)S(1)} %iota_multiply_fusion, s32[32]{0:T(128)S(1)} %iota_multiply_fusion.1, s32[64]{0:T(128)} %param.16), kind=kLoop, calls=%fused_computation.8 | loop fusion | flops 10240 | bytes 8832 | tf_op jit(solution)/shard_map/jit(_where)/select_n | solution.py:534
  3.3 1.4 %copy.12.table_ref = s32[64,32]{1,0:T(8,128)} copy(s32[64,32]{0,1:T(8,128)} %param.17) | data formatting | bytes 16384 | tf_op args[8]
  4.8 0.8 multiply_sine_fusion.1
  5.6 1.0 multiply_sine_fusion
  6.6 1.6 %copy.11 = bf16[2,2,128,128]{3,2,1,0:T(8,128)(2,1)} copy(bf16[2,2,128,128]{3,0,1,2:T(2,128)(2,1)} %bitcast.18) | data formatting | bytes 262144 | tf_op jit(solution)/shard_map/transpose | solution.py:538
  8.1 46.7 %gather.1 = (bf16[4,32,5120]{2,1,0:T(8,128)(2,1)}, bf16[4,4,256,128]{3,2,1,0:T(8,128)(2,1)}, bf16[4,4,256,128]{3,2,1,0:T(8,128)(2,1)}, bf16[4,128,640]{2,1,0:T(8...) custom-call(bf16[32,5120]{1,0:T(8,128)(2,1)} %hid_ref.1, ...), custom_call_target="tpu_custom_call" | custom-call | tf_op jit(solution)/shard_map/gather/pallas_call | solution.py:238
  54.8 4.5 %fusion.5.kvp_ref = f32[2,128,256]{2,1,0:T(8,128)} fusion(bf16[128,5120,1]{1,0,2:T(8,128)(2,1)} %bitcast.20, bf16[5120,2,256]{2,1,0:T(2,128)(2,1)} %param.11, f32[2,256]{1,0:T(2,128)S(1)} %convert_element_type.27), kind=kOutput, calls=%fused_computation.3 | convolution fusion | flops 671154176 | bytes 6817792 | tf_op jit(solution)/shard_map/td,dsc->stc/dot_general | solution.py:548
  59.3 13.4 %attend.1 = (bf16[2,4,128,640]{3,2,1,0:T(8,128)(2,1)}, f32[2,4,8,640]{3,2,1,0:T(8,128)}, bf16[128,512]{1,0:T(8,128)(2,1)}) custom-call(s32[8,128]{1,0:T(8,128)} %get-tuple-element.12.codes, f32[2,128,256]{2,1,0:T(8,128)} %fusion.5.kvp_ref, bf16[4,128,640]{2,1,0:T(8,128)(2,1)} %get-tuple-element.14.qy_ref, bf16[4,128,640]{2,1,0:T(8,128)(2,1)} %get-tuple-element.15.qx_ref, ...), custom_call_target="tpu_custom_call" | custom-call | tf_op jit(solution)/shard_map/attend/pallas_call | solution.py:355
  72.6 0.0 copy-start
  72.7 42.5 %project.1 = bf16[32,5120]{1,0:T(8,128)(2,1)} custom-call(bf16[2,4,128,640]{3,2,1,0:T(8,128)(2,1)} %get-tuple-element.18.o_ref, f32[2,4,8,640]{3,2,1,0:T(8,128)} %get-tuple-element.19.st_ref, bf16[2,2,4,80,1280]{4,3,2,1,0:T(8,128)(2,1)} %get-tuple-element.20.w4_ref, bf16[32,5120]{1,0:T(8,128)(2,1)} %hid_ref.1), custom_call_target="tpu_custom_call" | custom-call | tf_op jit(solution)/shard_map/project/pallas_call | solution.py:513
  115.2 0.0 copy-done
  115.2 0.7 reshape.58
  115.9 1.7 %copy.21 = bf16[32,5120]{1,0:T(8,128)(2,1)} copy(bf16[32,5120]{1,0:T(8,128)(2,1)} %project.1) | data formatting | bytes 655360
  (4 shorter events, 0.0 us)
Async XLA Ops:
  72.6 42.5 %copy-start = (bf16[128,512]{1,0:T(8,128)(2,1)S(1)}, bf16[128,512]{1,0:T(8,128)(2,1)}, u32[]{:S(2)}) copy-start(bf16[128,512]{1,0:T(8,128)(2,1)} %get-tuple-element.21) | copy-start | bytes 393220

commit v4 on v3

--- a/solution.py
+++ b/solution.py
@@ -46,15 +46,24 @@
         return self.at(s).at[pl.ds(h * self.half, self.half)]
 
     def start(self):
-        for n, by in ((0, 1), (1, -1)):
-            d = remote(self.own, self.at(self.me), self.sems, self.base + n, self.peer(by))
-            d.start()
-            self.sent.append(d)
+        for second in (0, 1):
+            for n, by in ((0, 1), (1, -1)):
+                h = n ^ second
+                src = self.own.at[pl.ds(h * self.half, self.half)]
+                d = remote(src, self.part(self.me, h), self.sems, self.base + 4 * second + n, self.peer(by))
+                d.start()
+                self.sent.append(d)
+
+    def landed(self, r, second):
+        n = 0 if r == -1 else 1
+        s = self.part(self.slot(r), n ^ second)
+        remote(s, s, self.sems, self.base + 4 * second + n, self.peer(1)).wait_recv()
 
     def arrived(self, r):
-        n = 0 if r == -1 else 1
-        s = self.at(self.slot(r))
-        remote(s, s, self.sems, self.base + n, self.peer(1)).wait_recv()
+        self.landed(r, 0)
+
+    def rest(self, r):
+        self.landed(r, 1)
 
     def forward(self, r):
         h = 0 if r == -1 else 1
@@ -73,8 +82,8 @@
             d.wait_send()
 
 
-def gather_kernel(rows_ref, pages_ref, q_ref, w_ref, gain_ref, table_ref, value_ref, normed, py, px, qy, qx, w4,
-                  codes, rows_all, sems, lsem):
+def gather_kernel(rows_ref, pages_ref, q_ref, w_ref, gain_ref, table_ref, lens_ref, inv_ref, normed, py, px, qy, qx, w4,
+                  codes, trig, rtrig, rows_all, sems, lsem):
     y, zh, x, zl, c = coords()
     partner = (y, zh, x, zl, 1 - c)
     across = (y, zh, x, 1 - zl, c)
@@ -87,7 +96,7 @@
     tp = 2 * zl + c
     base = [0]
 
-    def new(me, peer, own, at, half, count=4):
+    def new(me, peer, own, at, half, count=6):
         r = Ring(me, peer, own, at, half, sems, base[0])
         base[0] += count
         return r
@@ -130,13 +139,25 @@
             normed[slot, :, cols] = (v[:, k * 128:k * 128 + 128] * gain_ref[k:k + 1, :].astype(F32)).astype(BF)
 
     def find_codes():
-        table, value = table_ref[...], value_ref[...]
+        table = table_ref[...]
+        r = lax.broadcasted_iota(jnp.int32, (32, 64), 1)
+        j = lax.broadcasted_iota(jnp.int32, (32, 64), 0)
+        seen = jnp.clip(lens_ref[...] - j * 128, 0, 128)
+        value = jnp.where(seen > 0, r * 256 + seen, 0)
         row = lax.broadcasted_iota(jnp.int32, (64, 128), 0)
         lane = lax.broadcasted_iota(jnp.int32, (64, 128), 1)
         rows = [jnp.sum(jnp.where(table == p, value, 0), axis=0, keepdims=True) for p in range(64)]
         each = jnp.sum(jnp.concatenate(rows, axis=0), axis=1, keepdims=True)
         codes[0:1, :] = jnp.sum(jnp.where(row == lane, each, 0), axis=0, keepdims=True)
         codes[1:8, :] = jnp.zeros((7, 128), jnp.int32)
+
+    def find_tables():
+        own = lax.broadcasted_iota(jnp.int32, (128, 128), 0).astype(F32) * inv_ref[...]
+        trig[0], trig[1] = jnp.cos(own), jnp.sin(own)
+        diagonal = lax.broadcasted_iota(jnp.int32, (64, 64), 0) == lax.broadcasted_iota(jnp.int32, (64, 64), 1)
+        column = jnp.sum(jnp.where(diagonal, lens_ref[...], 0), axis=1, keepdims=True)
+        start = column.astype(F32) * inv_ref[...]
+        rtrig[0], rtrig[1] = jnp.cos(start), jnp.sin(start)
 
     local = [
         pltpu.make_async_copy(w_ref, w_slot(zh), lsem.at[0]),
@@ -186,6 +207,7 @@
         for h in (0, 1):
             zp[h].arrived(r)
             zp[h].forward(r)
+            zp[h].rest(r)
             p_near.append(begin(p_ring(r, h)))
     step(w_own)
     for r in q_rings:
@@ -196,11 +218,13 @@
     for r in (-1, 1):
         zw.arrived(r)
         zw.forward(r)
+        zw.rest(r)
         w_near.append(begin(w_ring(r)))
     r_across.start()
     remote(mine, mine, sems, b + 1, partner).wait_recv()
     norm(mine[...], 2 * zl + 1 - c)
     find_codes()
+    find_tables()
     p_far = []
     for h in (0, 1):
         zp[h].far()
@@ -218,8 +242,10 @@
     step(w_far)
     remote(other, other, sems, b + 2, partner).wait_recv()
     norm(other[...], 2 * (1 - zl) + 1 - c)
-    for r in q_rings + p_own + [w_own] + late:
-        r.far()
+    for ring in q_rings + p_own + [w_own] + late:
+        ring.rest(-1)
+        ring.rest(1)
+        ring.far()
     for r in rings + late:
         r.drain()
     for d in (r_across, r_partner, r_pass):
@@ -229,31 +255,31 @@
     assert base[0] <= NSEM, base[0]
 
 
-NSEM = 96
-
-
-def gather(rows, pages, q, w, gain, table, value):
+NSEM = 112
+
+
+def gather(rows, pages, q, w, gain, table, lens, inverse):
     s = jax.ShapeDtypeStruct
     vm = pl.BlockSpec(memory_space=pltpu.VMEM)
     return pl.pallas_call(
         gather_kernel,
         out_shape=(s((4, 32, 5120), BF), s((4, 4, 256, 128), BF), s((4, 4, 256, 128), BF),
                    s((4, 128, 640), BF), s((4, 128, 640), BF), s((2, 2, 4, 80, 1280), BF),
-                   s((8, 128), jnp.int32)),
-        in_specs=[vm] * 7,
-        out_specs=[vm] + [pl.BlockSpec(memory_space=pl.ANY)] * 5 + [vm],
+                   s((8, 128), jnp.int32), s((2, 128, 128), F32), s((2, 64, 128), F32)),
+        in_specs=[vm] * 8,
+        out_specs=[vm] + [pl.BlockSpec(memory_space=pl.ANY)] * 5 + [vm] * 3,
         scratch_shapes=[pltpu.VMEM((4, 32, 5120), BF), pltpu.SemaphoreType.DMA((2, NSEM)),
                         pltpu.SemaphoreType.DMA((5,))],
         compiler_params=pltpu.CompilerParams(collective_id=0, has_side_effects=True),
         name="gather",
-    )(rows, pages, q, w, gain, table, value)
+    )(rows, pages, q, w, gain, table, lens, inverse)
 
 
 NT = (((1,), (1,)), ((), ()))
 TN = (((0,), (0,)), ((), ()))
 
 
-def attend_kernel(codes, kvp_ref, qy_ref, qx_ref, py_ref, px_ref, cos_ref, sin_ref, rcos_ref, rsin_ref,
+def attend_kernel(codes, kvp_ref, bias_ref, qy_ref, qx_ref, py_ref, px_ref, trig_ref, rtrig_ref,
                   o_ref, st_ref, kv_ref, q_s, m_s, l_s, acc_s):
     y, zh, x, zl, c = coords()
     me = y * 16 + zh * 4 + x
@@ -262,18 +288,20 @@
     sign = jnp.where(lane < 64, -1.0, 1.0).astype(F32)
 
     def trig(r):
-        cl = rcos_ref[pl.ds(r, 1), :]
-        sl = rsin_ref[pl.ds(r, 1), :]
-        ct, st = cos_ref[...], sin_ref[...]
+        cl = rtrig_ref[0, pl.ds(r, 1), :]
+        sl = rtrig_ref[1, pl.ds(r, 1), :]
+        ct, st = trig_ref[0], trig_ref[1]
         return cl * ct - sl * st, (sl * ct + cl * st) * sign
 
     def rope(v, cs):
         return v * cs[0] + pltpu.roll(v, 64, 1) * cs[1]
 
     cs_own = trig(me)
+    bias = bias_ref[...].astype(F32)
     for h in range(2):
-        kv_ref[:, h * 128:(h + 1) * 128] = rope(kvp_ref[0, :, h * 128:(h + 1) * 128], cs_own).astype(BF)
-    kv_ref[:, 256:512] = kvp_ref[1].astype(BF)
+        key = kvp_ref[0, :, h * 128:(h + 1) * 128] + bias[0:1, h * 128:(h + 1) * 128]
+        kv_ref[:, h * 128:(h + 1) * 128] = rope(key, cs_own).astype(BF)
+    kv_ref[:, 256:512] = (kvp_ref[1] + bias[1:2, :]).astype(BF)
 
     row = lax.broadcasted_iota(jnp.int32, (128, 640), 0)
     col = lax.broadcasted_iota(jnp.int32, (128, 640), 1)
@@ -306,7 +334,7 @@
                 code = codes[0, page_of(s)]
                 return n + jnp.where((code // 256 == r) & (code % 256 > 0), 1, 0)
 
-            pages = lax.fori_loop(0, 16, count, jnp.int32(0))
+            pages = lax.fori_loop(0, 16, count, jnp.int32(0), unroll=True)
             active = (pages > 0) | (i == mine)
             m_s[...] = jnp.full_like(m_s, LOW)
             l_s[...] = jnp.zeros_like(l_s)
@@ -348,22 +376,22 @@
         lax.fori_loop(0, 4, one, 0)
 
 
-def attend(codes, kvp, qy, qx, py, px, trigs):
+def attend(codes, kvp, bias, qy, qx, py, px, trig, rtrig):
     s = jax.ShapeDtypeStruct
     vm = pl.BlockSpec(memory_space=pltpu.VMEM)
     sm = pl.BlockSpec(memory_space=pltpu.SMEM)
     return pl.pallas_call(
         attend_kernel,
         out_shape=(s((2, 4, 128, 640), BF), s((2, 4, 8, 640), F32), s((128, 512), BF)),
-        in_specs=[sm] + [vm] * 9,
+        in_specs=[sm] + [vm] * 8,
         out_specs=[vm] * 3,
         scratch_shapes=[pltpu.VMEM((640, 128), BF), pltpu.VMEM((8, 640), F32), pltpu.VMEM((8, 640), F32),
                         pltpu.VMEM((128, 640), F32)],
         name="attend",
-    )(codes, kvp, qy, qx, py.reshape(16, 256, 128), px.reshape(16, 256, 128), *trigs)
-
-
-def project_kernel(o_ref, st_ref, w4_ref, hid_ref, out_ref, fin, wv, ro, rst, relay, att, ay, ax, part, rc, ps, ra, tot, sems, wsem):
+    )(codes, kvp, bias, qy, qx, py.reshape(16, 256, 128), px.reshape(16, 256, 128), trig, rtrig)
+
+
+def project_kernel(o_ref, st_ref, w4_ref, out_ref, fin, wv, ro, rst, relay, att, ay, ax, part, rc, ps, ra, tot, sems, wsem):
     y, zh, x, zl, c = coords()
     partner = (y, zh, x, zl, 1 - c)
     across = (y, zh, x, 1 - zl, c)
@@ -432,7 +460,7 @@
     rings = []
     for t in range(2):
         rings.append(Ring(mine[t], functools.partial(shifted, axes[t]), att, (lambda s, t=t: bufs[t].at[s]), 64,
-                          sems, take(4)))
+                          sems, take(6)))
         rings[t].start()
     for d in load:
         d.wait()
@@ -473,8 +501,12 @@
             ring.arrived(r)
             ring.forward(r)
     pair(0)
+    for ring in rings:
+        ring.rest(-1)
     multiply(1)
     pair(1)
+    for ring in rings:
+        ring.rest(1)
     multiply(2)
     pair(2)
     finish(0)
@@ -495,8 +527,7 @@
                 first = g * 320 + u * 80
                 pieces.append(fin[1, s].astype(F32)[:, first:first + 80])
             cols = pl.ds(u * 1280 + g * 640, 640)
-            summed = jnp.concatenate(pieces, axis=1)
-            out_ref[:, cols] = (hid_ref[:, cols].astype(F32) + summed).astype(BF)
+            out_ref[:, cols] = jnp.concatenate(pieces, axis=1).astype(BF)
     for d in sent:
         d.wait_send()
     for ring in rings:
@@ -507,13 +538,13 @@
 NSEM3 = 56
 
 
-def project(o, st, w4, hidden):
+def project(o, st, w4):
     s = jax.ShapeDtypeStruct
     vm = pl.BlockSpec(memory_space=pltpu.VMEM)
     return pl.pallas_call(
         project_kernel,
         out_shape=s((32, 5120), BF),
-        in_specs=[vm, vm, pl.BlockSpec(memory_space=pl.ANY), vm],
+        in_specs=[vm, vm, pl.BlockSpec(memory_space=pl.ANY)],
         out_specs=vm,
         scratch_shapes=[
             pltpu.VMEM((2, 4, 32, 640), BF),
@@ -524,31 +555,21 @@
             pltpu.SemaphoreType.DMA((2, NSEM3)), pltpu.SemaphoreType.DMA((2,))],
         compiler_params=pltpu.CompilerParams(collective_id=1, has_side_effects=True),
         name="project",
-    )(o, st, w4, hidden)
-
-
-def entry_values(cached_len, shape):
-    r = lax.broadcasted_iota(jnp.int32, shape, 0)
-    j = lax.broadcasted_iota(jnp.int32, shape, 1)
-    seen = jnp.clip(cached_len[:, None] - j * 128, 0, 128)
-    return jnp.where(seen > 0, r * 256 + seen, 0)
+    )(o, st, w4)
 
 
 def local(hidden_in, norm_gain, kv_weight, kv_bias, queries, cache_pages, out_weight, cached_len, page_table):
     pages = cache_pages[0].transpose(2, 1, 0, 3).reshape(2, 256, 128)
-    normed, py, px, qy, qx, w4, codes = gather(
-        hidden_in, pages, queries, out_weight.T, norm_gain.reshape(40, 128),
-        page_table, entry_values(cached_len, page_table.shape))
     pair = lax.broadcasted_iota(jnp.int32, (1, 128), 1) % 64
     inverse = jnp.power(THETA, -pair.astype(F32) * 2.0 / 128)
-    trigs = []
-    for positions in (jnp.arange(128), cached_len):
-        angles = positions.astype(F32)[:, None] * inverse
-        trigs += [jnp.cos(angles), jnp.sin(angles)]
+    normed, py, px, qy, qx, w4, codes, trig, rtrig = gather(
+        hidden_in, pages, queries, out_weight.T, norm_gain.reshape(40, 128),
+        page_table.T, cached_len.reshape(1, 64), inverse)
     kvp = jnp.einsum("td,dsc->stc", normed.reshape(128, 5120), kv_weight, preferred_element_type=F32)
-    kvp = kvp + kv_bias.astype(F32)[:, None, :]
-    o, st, kv = attend(codes, kvp, qy, qx, py, px, trigs)
-    return project(o, st, w4, hidden_in), kv.reshape(128, 2, 2, 128)
+    o, st, kv = attend(codes, kvp, kv_bias, qy, qx, py, px, trig, rtrig)
+    summed = project(o, st, w4)
+    hidden_out = (hidden_in.astype(F32) + summed.astype(F32)).astype(BF)
+    return hidden_out, kv.reshape(128, 2, 2, 128)
 
 
 def solution(mesh):

time: 118 us -> 111 us (0.941)
  the two profiles are of different devices: /device:TPU:64 before, /device:TPU:66 now
where the time goes in v4:
time: 111 us
  Pallas kernels  101 us (91%)
  matrix products  4.46 us (4%)
  other arithmetic  2.3 us (2%)
  local copies, waits for them, and re-layouts  2.27 us (2%)
    pallas_call x1, Pallas kernels, gather(): pl.pallas_call(gather_kernel, out_shape=(s((4, 32, 5120), BF), s((4, 4, 2...  45.8 us
    pallas_call x1, Pallas kernels, project(): pl.pallas_call(project_kernel, out_shape=s((32, 5120), BF), in_specs=[vm,...  43.8 us
    pallas_call x1, Pallas kernels, attend(): pl.pallas_call(attend_kernel, out_shape=(s((2, 4, 128, 640), BF), s((2, 4...  11.4 us
    dot_general x1, matrix products, local(): jnp.einsum('td,dsc->stc', normed.reshape(128, 5120), kv_weight, preferred...  4.46 us

profile of v4, /device:TPU:66, one launch (start us, length us, event | category | flops | bytes accessed | tf_op | source)
XLA Modules:
  0.0 110.7 jit_solution(12494863620410851114)
XLA Ops:
  0.6 0.5 fusion.8.inv_ref
  1.2 1.6 %copy.11 = bf16[2,2,128,128]{3,2,1,0:T(8,128)(2,1)} copy(bf16[2,2,128,128]{3,0,1,2:T(2,128)(2,1)} %bitcast.20) | data formatting | bytes 262144 | tf_op jit(solution)/shard_map/transpose | solution.py:562
  2.7 45.8 %gather.1 = (bf16[4,32,5120]{2,1,0:T(8,128)(2,1)}, bf16[4,4,256,128]{3,2,1,0:T(8,128)(2,1)}, bf16[4,4,256,128]{3,2,1,0:T(8,128)(2,1)}, bf16[4,128,640]{2,1,0:T(8...) custom-call(bf16[32,5120]{1,0:T(8,128)(2,1)} %rows_ref.1, ...), custom_call_target="tpu_custom_call" | custom-call | tf_op jit(solution)/shard_map/gather/pallas_call | solution.py:264
  48.5 4.5 %fusion.2.kvp_ref = f32[2,128,256]{2,1,0:T(8,128)} fusion(bf16[128,5120,1]{1,0,2:T(8,128)(2,1)} %bitcast.24, bf16[5120,2,256]{2,1,0:T(2,128)(2,1)} %param.11), kind=kOutput, calls=%fused_computation.2 | convolution fusion | flops 671088640 | bytes 6815744 | tf_op jit(solution)/shard_map/td,dsc->stc/dot_general | solution.py:568
  53.0 11.4 %attend.1 = (bf16[2,4,128,640]{3,2,1,0:T(8,128)(2,1)}, f32[2,4,8,640]{3,2,1,0:T(8,128)}, bf16[128,512]{1,0:T(8,128)(2,1)}) custom-call(s32[8,128]{1,0:T(8,128)} %get-tuple-element.14.codes, f32[2,128,256]{2,1,0:T(8,128)} %fusion.2.kvp_ref, bf16[2,256]{1,0:T(2,128)(2,1)} %bias_ref.1, bf16[4,128,640]{2,1,0:T(8,128)(2,1)} %get-tuple-element.16.qy_ref, ...), custom_call_target="tpu_custom_call" | custom-call | tf_op jit(solution)/shard_map/attend/pallas_call | solution.py:383
  64.4 0.0 copy-start
  64.4 0.0 copy-start.1
  64.4 43.8 %project.1 = bf16[32,5120]{1,0:T(8,128)(2,1)} custom-call(bf16[2,4,128,640]{3,2,1,0:T(8,128)(2,1)} %get-tuple-element.22.o_ref, f32[2,4,8,640]{3,2,1,0:T(8,128)} %get-tuple-element.23.st_ref, bf16[2,2,4,80,1280]{4,3,2,1,0:T(8,128)(2,1)} %get-tuple-element.24.w4_ref), custom_call_target="tpu_custom_call" | custom-call | tf_op jit(solution)/shard_map/project/pallas_call | solution.py:544
  108.2 0.0 copy-done
  108.2 1.8 %add_convert_fusion = bf16[32,5120]{1,0:T(8,128)(2,1)} fusion(bf16[32,5120]{1,0:T(8,128)(2,1)} %project.1, bf16[32,5120]{1,0:T(8,128)(2,1)S(1)} %copy-done), kind=kLoop, calls=%fused_computation.3 | loop fusion | flops 655360 | bytes 983040 | tf_op jit(solution)/shard_map/convert_element_type | solution.py:571
  110.0 0.0 copy-done.1
  110.0 0.7 reshape.76
Async XLA Ops:
  64.4 43.8 %copy-start = (bf16[32,5120]{1,0:T(8,128)(2,1)S(1)}, bf16[32,5120]{1,0:T(8,128)(2,1)}, u32[]{:S(2)}) copy-start(bf16[32,5120]{1,0:T(8,128)(2,1)} %rows_ref.1) | copy-start | bytes 983044
  64.4 45.6 %copy-start.1 = (bf16[128,512]{1,0:T(8,128)(2,1)S(1)}, bf16[128,512]{1,0:T(8,128)(2,1)}, u32[]{:S(2)}) copy-start(bf16[128,512]{1,0:T(8,128)(2,1)} %get-tuple-element.25) | copy-start | bytes 393220

commit v5 on v4

--- a/solution.py
+++ b/solution.py
@@ -270,7 +270,7 @@
         out_specs=[vm] + [pl.BlockSpec(memory_space=pl.ANY)] * 5 + [vm] * 3,
         scratch_shapes=[pltpu.VMEM((4, 32, 5120), BF), pltpu.SemaphoreType.DMA((2, NSEM)),
                         pltpu.SemaphoreType.DMA((5,))],
-        compiler_params=pltpu.CompilerParams(collective_id=0, has_side_effects=True),
+        compiler_params=pltpu.CompilerParams(collective_id=0, has_side_effects=True, vmem_limit_bytes=12 * 2**20),
         name="gather",
     )(rows, pages, q, w, gain, table, lens, inverse)
 
@@ -387,6 +387,7 @@
         out_specs=[vm] * 3,
         scratch_shapes=[pltpu.VMEM((640, 128), BF), pltpu.VMEM((8, 640), F32), pltpu.VMEM((8, 640), F32),
                         pltpu.VMEM((128, 640), F32)],
+        compiler_params=pltpu.CompilerParams(vmem_limit_bytes=16 * 2**20),
         name="attend",
     )(codes, kvp, bias, qy, qx, py.reshape(16, 256, 128), px.reshape(16, 256, 128), trig, rtrig)
 
@@ -553,7 +554,7 @@
             pltpu.VMEM((4, 128, 1280), BF), pltpu.VMEM((2, 4, 2, 2, 32, 640), BF), pltpu.VMEM((2, 4, 2, 32, 640), BF),
             pltpu.VMEM((2, 4, 32, 640), BF), pltpu.VMEM((2, 4, 32, 640), BF), pltpu.VMEM((2, 4, 32, 640), BF),
             pltpu.SemaphoreType.DMA((2, NSEM3)), pltpu.SemaphoreType.DMA((2,))],
-        compiler_params=pltpu.CompilerParams(collective_id=1, has_side_effects=True),
+        compiler_params=pltpu.CompilerParams(collective_id=1, has_side_effects=True, vmem_limit_bytes=24 * 2**20),
         name="project",
     )(o, st, w4)
 

time: 111 us -> 106 us (0.955)
  the two profiles are of different devices: /device:TPU:66 before, /device:TPU:1 now
where the time goes in v5:
time: 106 us
  Pallas kernels  94.5 us (89%)
  local copies, waits for them, and re-layouts  6.57 us (6%)
  matrix products  3.34 us (3%)
    pallas_call x1, Pallas kernels, project(): pl.pallas_call(project_kernel, out_shape=s((32, 5120), BF), in_specs=[vm,...  46.8 us
    pallas_call x1, Pallas kernels, gather(): pl.pallas_call(gather_kernel, out_shape=(s((4, 32, 5120), BF), s((4, 4, 2...  43.9 us
    unnamed x16, local copies, waits for them, and re-layouts  4.96 us
    pallas_call x1, Pallas kernels, attend(): pl.pallas_call(attend_kernel, out_shape=(s((2, 4, 128, 640), BF), s((2, 4...  3.82 us
    dot_general x1, matrix products, local(): jnp.einsum('td,dsc->stc', normed.reshape(128, 5120), kv_weight, preferred...  3.34 us

profile of v5, /device:TPU:1, one launch (start us, length us, event | category | flops | bytes accessed | tf_op | source)
XLA Modules:
  0.0 106.0 jit_solution(13344412584923640613)
XLA Ops:
  0.6 0.9 copy.11
  1.6 0.0 copy-start
  1.6 1.0 copy-done
  2.5 0.0 copy-start.2
  2.5 1.0 copy-done.2
  3.5 0.0 copy-start.3
  3.5 0.9 copy-done.3
  4.5 0.0 copy-start.4
  4.5 0.7 copy-done.4
  5.2 0.0 copy-start.5
  5.2 0.7 copy-done.5
  5.9 0.0 copy-start.7
  5.9 0.7 copy-done.7
  6.5 43.9 %gather.1 = (bf16[4,32,5120]{2,1,0:T(8,128)(2,1)S(1)}, bf16[4,4,256,128]{3,2,1,0:T(8,128)(2,1)S(1)}, bf16[4,4,256,128]{3,2,1,0:T(8,128)(2,1)S(1)}, bf16[4,128,64...) custom-call(bf16[32,5120]{1,0:T(8,128)(2,1)S(1)} %copy-done, ...), custom_call_target="tpu_custom_call" | custom-call | tf_op jit(solution)/shard_map/gather/pallas_call | solution.py:264
  50.4 0.0 copy-start.6
  50.5 3.3 %fusion.2.kvp_ref = f32[2,128,256]{2,1,0:T(8,128)S(1)} fusion(bf16[128,5120,1]{1,0,2:T(8,128)(2,1)S(1)} %bitcast.23, bf16[5120,2,256]{2,1,0:T(2,128)(2,1)} %param.11), kind=kOutput, calls=%fused_computation.2 | convolution fusion | flops 671088640 | bytes 6815744 | tf_op jit(solution)/shard_map/td,dsc->stc/dot_general | solution.py:569
  53.8 0.0 copy-done.6
  53.8 3.8 %attend.1 = (bf16[2,4,128,640]{3,2,1,0:T(8,128)(2,1)S(1)}, f32[2,4,8,640]{3,2,1,0:T(8,128)S(1)}, bf16[128,512]{1,0:T(8,128)(2,1)S(1)}) custom-call(s32[8,128]{1,0:T(8,128)S(1)} %get-tuple-element.14.codes, f32[2,128,256]{2,1,0:T(8,128)S(1)} %fusion.2.kvp_ref, bf16[2,256]{1,0:T(2,128)(2,1)S(1)} %copy-done.6, ...), custom_call_target="tpu_custom_call" | custom-call | tf_op jit(solution)/shard_map/attend/pallas_call | solution.py:383
  57.6 0.0 copy-start.1
  57.6 46.8 %project.1 = bf16[32,5120]{1,0:T(8,128)(2,1)S(1)} custom-call(bf16[2,4,128,640]{3,2,1,0:T(8,128)(2,1)S(1)} %get-tuple-element.22.o_ref, f32[2,4,8,640]{3,2,1,0:T(8,128)S(1)} %get-tuple-element.23.st_ref, bf16[2,2,4,80,1280]{4,3,2,1,0:T(8,128)(2,1)S(1)} %get-tuple-element.24.w4_ref), custom_call_target="tpu_custom_call" | custom-call | tf_op jit(solution)/shard_map/project/pallas_call | solution.py:545
  104.5 0.0 copy-done.1
  104.5 0.8 add_convert_fusion
  105.3 0.7 reshape.76
  (1 shorter events, 0.0 us)
Async XLA Ops:
  1.6 1.0 copy-start
  2.5 1.0 copy-start.2
  3.5 0.9 copy-start.3
  4.5 0.7 copy-start.4
  5.2 0.7 copy-start.5
  5.9 0.7 copy-start.7
  50.4 3.4 %copy-start.6 = (bf16[2,256]{1,0:T(2,128)(2,1)S(1)}, bf16[2,256]{1,0:T(2,128)(2,1)}, u32[]{:S(2)}) copy-start(bf16[2,256]{1,0:T(2,128)(2,1)} %bias_ref.1) | copy-start | bytes 3076
  57.6 46.8 %copy-start.1 = (bf16[32,5120]{1,0:T(8,128)(2,1)S(1)}, bf16[32,5120]{1,0:T(8,128)(2,1)}, u32[]{:S(2)}) copy-start(bf16[32,5120]{1,0:T(8,128)(2,1)} %rows_ref.1) | copy-start | bytes 983044
